TPU v7x, 32 devices: a whole 2x2x4 slice. The times are simulated.
32 devices in a mesh: row: 8 (over z, x), col: 4 (over y, core).
Axes of the slice: x: 2, y: 2, z: 4, core: 2. Of those that a mesh axis runs over, the one named last changes fastest.
Arguments:
- affinity: bfloat16 [32768, 8192], P('row', 'col'), may hold values from -250 to 250
- seed_values: int32 [16], replicated, may hold values from 0 to 1073741823
- sku_ids: int32 [8192], P('col'), may hold values from 0 to 8191, each once
Outputs:
- range_basis: float32 [16, 32768], P(None, ('row', 'col'))
- range_factor: float32 [16, 16], replicated
All inputs are finite; a program needn't handle non-finite values.
Results may differ from a plain program's by a relative error of at most 0.0046.
Values may be sent and summed in bfloat16 or wider, within the bound.
A program may use at most 64 MiB of HBM per device.

v0:
```python
import functools
import math

import jax
import jax.numpy as jnp
from jax import lax
from jax.experimental import pallas as pl
from jax.experimental.pallas import tpu as pltpu
from jax.sharding import PartitionSpec as P

ITERS = 2
SUB = 2
DEPTH = 3
HIGHEST = lax.Precision.HIGHEST
MESH = pl.DeviceIdType.MESH

mix_first = -2048144789
mix_second = -1028477387
golden = -1640531535
salt_value = 1540483477


def shifted(value, amount):
    return lax.shift_right_logical(value, jnp.full(value.shape, amount, jnp.int32))


def scramble(value):
    value = jnp.bitwise_xor(value, shifted(value, 16))
    value = value * jnp.int32(mix_first)
    value = jnp.bitwise_xor(value, shifted(value, 13))
    value = value * jnp.int32(mix_second)
    return jnp.bitwise_xor(value, shifted(value, 16))


def test_matrix(seeds, skus, total_columns):
    first = scramble(jnp.bitwise_xor(seeds, skus * jnp.int32(golden)))
    second = scramble(jnp.bitwise_xor(first, jnp.int32(salt_value)))
    uniform_a = (shifted(first, 9) + 1).astype(jnp.float32) / 8388608.0
    uniform_b = (shifted(second, 9) + 1).astype(jnp.float32) / 8388608.0
    gauss = jnp.sqrt(-2.0 * jnp.log(uniform_a)) * jnp.cos(6.283185307179586 * uniform_b)
    return (gauss / math.sqrt(total_columns)).astype(jnp.bfloat16)


def factorize(gram):
    count = gram.shape[0]
    rows = lax.broadcasted_iota(jnp.int32, (count, count), 0)
    cols = lax.broadcasted_iota(jnp.int32, (count, count), 1)
    left = gram
    right = (rows == cols).astype(jnp.float32)
    for j in range(count):
        pivot = left[j : j + 1, j : j + 1]
        inv = lax.rsqrt(pivot)
        inv = inv * (1.5 - 0.5 * (pivot * inv) * inv)
        left_row = left[j : j + 1, :] * inv
        right_row = right[j : j + 1, :] * inv
        factor = left[:, j : j + 1] * inv
        left = jnp.where(rows == j, left_row, jnp.where(rows > j, left - factor * left_row, left))
        right = jnp.where(rows == j, right_row, jnp.where(rows > j, right - factor * right_row, right))
    return jnp.where(rows <= cols, left, 0.0), right


def kernel(
    dims,
    slab_hbm, seed_ref, sku_ref,
    basis_ref, factor_ref,
    slab, slab_t, x_ref, part, half_recv, y_sum, part_last, recv_last, s_ref, lhs, zacc, zpart, zrecv, back,
    gsend_row, grecv_row, grecv_col, gcol, gram_part, mine,
    load_sem, a_send_sem, a_recv_sem, y_send_sem, y_recv_sem, last_send_sem, last_recv_sem, s_send_sem, s_recv_sem,
    z_send_sem, z_recv_sem, b_send_sem, b_recv_sem, g_send_sem, g_recv_sem, c_send_sem, c_recv_sem,
):
    R, C, K, piece, width, inv_root, scale = dims
    w = width // R
    me_r = lax.axis_index("row")
    me_c = lax.axis_index("col")

    Y = C // 2
    core, me_y = lax.rem(me_c, 2), me_c // 2
    partner = me_y * 2 + (1 - core)

    def y_peer(k):
        return lax.rem(me_y + k, Y) * 2 + core

    def col_peer_of(k):
        return (1 - core) * Y + k if k < Y else core * Y + k - Y

    def row_peer(k):
        return lax.rem(me_r + k, R)

    def row_from(k):
        return lax.rem(me_r + (R - k), R)

    span = piece // SUB
    n_load = C * SUB

    def load(i):
        start = col_peer_of(i // SUB) * piece + (i % SUB) * span
        return pltpu.make_async_copy(
            slab_hbm.at[pl.ds(pl.multiple_of(start, span), span), :],
            slab.at[i // SUB, pl.ds((i % SUB) * span, span), :],
            load_sem.at[i],
        )

    for i in range(min(DEPTH, n_load)):
        load(i).start()

    barrier = pltpu.get_barrier_semaphore()
    for k in range(1, R):
        pl.semaphore_signal(barrier, inc=1, device_id={"row": row_peer(k)}, device_id_type=MESH)
    for k in range(1, C):
        pl.semaphore_signal(barrier, inc=1, device_id={"col": lax.rem(me_c + k, C)}, device_id_type=MESH)

    index = lax.broadcasted_iota(jnp.int32, (K, width), 0)
    seeds = jnp.zeros((K, width), jnp.int32)
    for k in range(K):
        seeds = jnp.where(index == k, seed_ref[k], seeds)
    x_ref[...] = test_matrix(seeds, jnp.broadcast_to(sku_ref[...], (K, width)), width * C)

    pl.semaphore_wait(barrier, (R - 1) + (C - 1))

    pending = []

    def col_copy(src, dst, send, recv, target):
        return pltpu.make_async_remote_copy(
            src_ref=src, dst_ref=dst, send_sem=send, recv_sem=recv,
            device_id={"col": lax.rem(target, C)}, device_id_type=MESH,
        )

    def row_copy(src, dst, send, recv, k):
        return pltpu.make_async_remote_copy(
            src_ref=src, dst_ref=dst, send_sem=send, recv_sem=recv,
            device_id={"row": row_peer(k)}, device_id_type=MESH,
        )

    def project(k):
        return jnp.dot(x_ref[...], slab_t[k], preferred_element_type=jnp.float32)

    def position(c):
        half = c // Y
        same = 1 - (half + core - 2 * half * core)
        return lax.rem(c, Y) + Y * same

    def send_half(it, q):
        copy = col_copy(
            part.at[it, q], half_recv.at[it, q], a_send_sem.at[it, q], a_recv_sem.at[it, q], partner
        )
        copy.start()
        pending.append(copy)

    def send_y(it, q, value):
        col_copy(
            part.at[it, q], half_recv.at[it, q], a_send_sem.at[it, q], a_recv_sem.at[it, q], partner
        ).wait_recv()
        y_sum[it, q, me_y] = value + half_recv[it, q]
        for k in range(1, Y):
            copy = col_copy(
                y_sum.at[it, q, me_y], y_sum.at[it, q, me_y],
                y_send_sem.at[it, q, k], y_recv_sem.at[it, q, k], y_peer(k),
            )
            copy.start()
            pending.append(copy)

    def square(value):
        return lax.dot_general(
            value, value, (((1,), (1,)), ((), ())), precision=HIGHEST, preferred_element_type=jnp.float32
        )

    for it in range(ITERS + 1):
        if it == ITERS:
            copies = []
            for k in list(range(2, C)) + [1]:
                target = lax.rem(me_y + k // 2, Y) * 2 + (1 - core if k % 2 else core)
                part_last[k] = project(position(target))
                copy = col_copy(
                    part_last.at[k], recv_last.at[k], last_send_sem.at[k], last_recv_sem.at[k], target
                )
                copy.start()
                copies.append(copy)
            own = project(position(me_c))
            for k in [1] + list(range(2, C)):
                copies[(k - 2) % (C - 1)].wait_recv()
                own = own + recv_last[k]
            pending += copies
            own = own * inv_root
            gram = square(own)
            gcol[...] = gram
            copies = []
            for k in range(1, C):
                copy = col_copy(gcol, grecv_col.at[me_c], c_send_sem.at[k], c_recv_sem.at[k], me_c + k)
                copy.start()
                copies.append(copy)
            grecv_col[me_c] = gram
            for k in range(1, C):
                source = lax.rem(me_c + (C - k), C)
                col_copy(
                    gcol, grecv_col.at[source], c_send_sem.at[k], c_recv_sem.at[k], me_c + k
                ).wait_recv()
            pending += copies
            gram = grecv_col[0]
            for c in range(1, C):
                gram = gram + grecv_col[c]
        else:
            if it == 0:
                for i in range(n_load + 1):
                    if i < n_load:
                        load(i).wait()
                        if i + DEPTH < n_load:
                            load(i + DEPTH).start()
                        here = slice((i % SUB) * span, (i % SUB + 1) * span)
                        slab_t[i // SUB, :, here] = slab[i // SUB, here, :].T
                    if i > 0:
                        k, sub = (i - 1) // SUB, (i - 1) % SUB
                        here = slice(sub * span, (sub + 1) * span)
                        value = jnp.dot(x_ref[...], slab_t[k, :, here], preferred_element_type=jnp.float32)
                        if k < Y:
                            part[it, k, :, here] = value
                            if sub == SUB - 1:
                                send_half(it, k)
                        else:
                            mine[:, here] = value
                            if sub == SUB - 1:
                                send_y(it, k - Y, mine[...])
            else:
                for q in range(Y):
                    part[it, q] = project(q)
                    send_half(it, q)
                for q in range(Y):
                    send_y(it, q, project(Y + q))
            gram = None
            for q in range(C):
                at = Y + q if q < Y else q - Y
                if q < Y:
                    c = core * Y + q
                    for k in range(1, Y):
                        source = lax.rem(me_y + (Y - k), Y)
                        col_copy(
                            y_sum.at[it, q, source], y_sum.at[it, q, source],
                            y_send_sem.at[it, q, k], y_recv_sem.at[it, q, k], y_peer(k),
                        ).wait_recv()
                    value = y_sum[it, q, 0]
                    for y in range(1, Y):
                        value = value + y_sum[it, q, y]
                    if it > 0:
                        value = value * inv_root
                    s_ref[it, c] = value
                    copy = col_copy(
                        s_ref.at[it, c], s_ref.at[it, c], s_send_sem.at[it, q], s_recv_sem.at[it, q], partner
                    )
                    copy.start()
                    pending.append(copy)
                else:
                    c = (1 - core) * Y + q - Y
                    col_copy(
                        s_ref.at[it, c], s_ref.at[it, c], s_send_sem.at[it, q - Y], s_recv_sem.at[it, q - Y], partner
                    ).wait_recv()
                    value = s_ref[it, c]
                high = value.astype(jnp.bfloat16)
                low = (value - high.astype(jnp.float32)).astype(jnp.bfloat16)
                lhs[:K, :] = high
                lhs[K:, :] = low
                if q < C - 1 or w % 128:
                    product = jnp.dot(lhs[...], slab[at], preferred_element_type=jnp.float32)
                    product = product[:K] + product[K:]
                    zacc[...] = product if q == 0 else zacc[...] + product
                gram_part[it, c] = square(value)
            gram = gram_part[it, 0]
            for c in range(1, C):
                gram = gram + gram_part[it, c]

        gsend_row[it] = gram
        for k in range(1, R):
            copy = row_copy(
                gsend_row.at[it], grecv_row.at[it, me_r], g_send_sem.at[it, k], g_recv_sem.at[it, k], k
            )
            copy.start()
            pending.append(copy)
        grecv_row[it, me_r] = gram

        if it < ITERS:
            last = Y - 1
            if w % 128:
                for r in range(R):
                    zpart[it, r] = zacc[:, r * w : (r + 1) * w]
            z_copies = []
            for k in list(range(1, R)) + [0]:
                r = row_peer(k)
                if w % 128 == 0:
                    cols = pl.ds(pl.multiple_of(r * w, w), w)
                    product = jnp.dot(lhs[...], slab[last, :, cols], preferred_element_type=jnp.float32)
                    zpart[it, r] = zacc[:, cols] + product[:K] + product[K:]
                if k > 0:
                    copy = row_copy(
                        zpart.at[it, r], zrecv.at[it, k], z_send_sem.at[it, k], z_recv_sem.at[it, k], k
                    )
                    copy.start()
                    z_copies.append((k, copy))

        for k in range(1, R):
            row_copy(
                gsend_row.at[it], grecv_row.at[it, row_from(k)], g_send_sem.at[it, k], g_recv_sem.at[it, k], k
            ).wait_recv()
        gram = grecv_row[it, 0]
        for r in range(1, R):
            gram = gram + grecv_row[it, r]
        upper, inverse = factorize(gram)

        if it == ITERS:
            ortho = jnp.dot(inverse, own, precision=HIGHEST, preferred_element_type=jnp.float32)
            basis_ref[...] = ortho * scale
            factor_ref[...] = upper / scale
        else:
            total = zpart[it, me_r]
            for k, copy in z_copies:
                copy.wait_recv()
                total = total + zrecv[it, k]
                pending.append(copy)
            back[it, me_r] = jnp.dot(
                inverse, total, precision=HIGHEST, preferred_element_type=jnp.float32
            ).astype(jnp.bfloat16)
            for k in range(1, R):
                copy = row_copy(
                    back.at[it, me_r], back.at[it, me_r], b_send_sem.at[it, k], b_recv_sem.at[it, k], k
                )
                copy.start()
                pending.append(copy)
            for k in range(1, R):
                r = row_from(k)
                row_copy(
                    back.at[it, r], back.at[it, r], b_send_sem.at[it, k], b_recv_sem.at[it, k], k
                ).wait_recv()
            for r in range(R):
                x_ref[:, r * w : (r + 1) * w] = back[it, r]

    for copy in pending:
        copy.wait_send()


def body(affinity, seed_values, sku_ids):
    R, C = lax.axis_size("row"), lax.axis_size("col")
    K = seed_values.shape[0]
    rows, width = affinity.shape
    piece, w, Y = rows // C, width // R, C // 2
    dims = (R, C, K, piece, width, 1.0 / math.sqrt(width * C), math.sqrt(rows * R))
    f32, bf16 = jnp.float32, jnp.bfloat16
    dma = pltpu.SemaphoreType.DMA
    vmem = pl.BlockSpec(memory_space=pltpu.VMEM)
    return pl.pallas_call(
        functools.partial(kernel, dims),
        out_shape=(
            jax.ShapeDtypeStruct((K, piece), f32),
            jax.ShapeDtypeStruct((K, K), f32),
        ),
        in_specs=[
            pl.BlockSpec(memory_space=pl.ANY),
            pl.BlockSpec(memory_space=pltpu.SMEM),
            vmem,
        ],
        out_specs=(vmem, vmem),
        scratch_shapes=[
            pltpu.VMEM((C, piece, width), bf16),
            pltpu.VMEM((C, width, piece), bf16),
            pltpu.VMEM((K, width), bf16),
            pltpu.VMEM((ITERS, Y, K, piece), f32),
            pltpu.VMEM((ITERS, Y, K, piece), f32),
            pltpu.VMEM((ITERS, Y, Y, K, piece), f32),
            pltpu.VMEM((C, K, piece), f32),
            pltpu.VMEM((C, K, piece), f32),
            pltpu.VMEM((ITERS, C, K, piece), f32),
            pltpu.VMEM((2 * K, piece), bf16),
            pltpu.VMEM((K, width), f32),
            pltpu.VMEM((ITERS, R, K, w), f32),
            pltpu.VMEM((ITERS, R, K, w), f32),
            pltpu.VMEM((ITERS, R, K, w), bf16),
            pltpu.VMEM((ITERS + 1, K, K), f32),
            pltpu.VMEM((ITERS + 1, R, K, K), f32),
            pltpu.VMEM((C, K, K), f32),
            pltpu.VMEM((K, K), f32),
            pltpu.VMEM((ITERS, C, K, K), f32),
            pltpu.VMEM((K, piece), f32),
            dma((C * SUB,)),
            dma((ITERS, Y)), dma((ITERS, Y)),
            dma((ITERS, Y, Y)), dma((ITERS, Y, Y)),
            dma((C,)), dma((C,)),
            dma((ITERS, Y)), dma((ITERS, Y)),
            dma((ITERS, R)), dma((ITERS, R)),
            dma((ITERS, R)), dma((ITERS, R)),
            dma((ITERS + 1, R)), dma((ITERS + 1, R)),
            dma((C,)), dma((C,)),
        ],
        compiler_params=pltpu.CompilerParams(
            collective_id=0, has_side_effects=True, vmem_limit_bytes=60 * 1024 * 1024
        ),
    )(affinity, seed_values, sku_ids[None, :])


def solution(mesh):
    placed = (P("row", "col"), P(), P("col"))
    return jax.shard_map(
        body, mesh=mesh, in_specs=placed, out_specs=(P(None, ("row", "col")), P()), check_vma=False
    )
```

profile of v0, /device:TPU:0, one launch (start us, length us, event | category | flops | bytes accessed | tf_op | source)
XLA Modules:
  0.0 66.3 jit_solution(7436596084420236882)
XLA Ops:
  0.6 62.9 %shard_map.50 = (f32[16,1024]{1,0:T(8,128)}, f32[16,16]{1,0:T(8,128)}) custom-call(bf16[4096,2048]{1,0:T(8,128)(2,1)} %slab_hbm.1, s32[16]{0:T(128)} %seed_ref.1, s32[1,2048]{1,0:T(1,128)} %bitcast.1), custom_call_target="tpu_custom_call" | custom-call | tf_op jit(solution)/shard_map/pallas_call | solution.py:346
  63.5 1.5 %copy.7 = f32[16,1024]{1,0:T(8,128)} copy(f32[16,1024]{1,0:T(8,128)} %get-tuple-element.4) | data formatting | bytes 131072
  65.0 1.3 %copy.8 = f32[16,16]{1,0:T(8,128)} copy(f32[16,16]{1,0:T(8,128)} %get-tuple-element.5) | data formatting | bytes 2048
where the time goes:
time: 66.6 us; the launch traced here: 66.3 us
  Pallas kernels  62.9 us (94%)
  local copies, waits for them, and re-layouts  2.77 us (4%)
    pallas_call x1, Pallas kernels, body(): pl.pallas_call(functools.partial(kernel, dims), out_shape=(jax.ShapeDtype...  62.9 us
    unnamed x2, local copies, waits for them, and re-layouts  2.77 us

commit v1 on v0

v1 whole, which is shorter than its diff:
```python
import functools
import math

import jax
import jax.numpy as jnp
from jax import lax
from jax.experimental import pallas as pl
from jax.experimental.pallas import tpu as pltpu
from jax.sharding import PartitionSpec as P

ITERS = 2
SUB = 2
DEPTH = 4
TASKS = ((0, 1, 2), (3, 4, 5), (6, 7))
HIGHEST = lax.Precision.HIGHEST
MESH = pl.DeviceIdType.MESH

mix_first = -2048144789
mix_second = -1028477387
golden = -1640531535
salt_value = 1540483477


def shifted(value, amount):
    return lax.shift_right_logical(value, jnp.full(value.shape, amount, jnp.int32))


def scramble(value):
    value = jnp.bitwise_xor(value, shifted(value, 16))
    value = value * jnp.int32(mix_first)
    value = jnp.bitwise_xor(value, shifted(value, 13))
    value = value * jnp.int32(mix_second)
    return jnp.bitwise_xor(value, shifted(value, 16))


def test_matrix(seeds, skus, total_columns):
    first = scramble(jnp.bitwise_xor(seeds, skus * jnp.int32(golden)))
    second = scramble(jnp.bitwise_xor(first, jnp.int32(salt_value)))
    uniform_a = (shifted(first, 9) + 1).astype(jnp.float32) / 8388608.0
    uniform_b = (shifted(second, 9) + 1).astype(jnp.float32) / 8388608.0
    gauss = jnp.sqrt(-2.0 * jnp.log(uniform_a)) * jnp.cos(6.283185307179586 * uniform_b)
    return (gauss / math.sqrt(total_columns)).astype(jnp.bfloat16)


def factorize(gram):
    count = gram.shape[0]
    rows = lax.broadcasted_iota(jnp.int32, (count, count), 0)
    cols = lax.broadcasted_iota(jnp.int32, (count, count), 1)
    left = gram
    right = (rows == cols).astype(jnp.float32)
    for j in range(count):
        pivot = left[j : j + 1, j : j + 1]
        inv = lax.rsqrt(pivot)
        inv = inv * (1.5 - 0.5 * (pivot * inv) * inv)
        left_row = left[j : j + 1, :] * inv
        right_row = right[j : j + 1, :] * inv
        factor = left[:, j : j + 1] * inv
        left = jnp.where(rows == j, left_row, jnp.where(rows > j, left - factor * left_row, left))
        right = jnp.where(rows == j, right_row, jnp.where(rows > j, right - factor * right_row, right))
    return jnp.where(rows <= cols, left, 0.0), right


def kernel(
    dims,
    slab_hbm, seed_hbm, sku_hbm,
    basis_ref, factor_ref,
    slab, slab_t, seed_ref, sku_ref, x_ref, acc, part, half_recv, y_sum, fin_part, fin_recv, fin_sum, fin_y,
    s_ref, lhs, zacc, zpart, zrecv, back,
    gsend_row, grecv_row, grecv_col, gcol, gram_part,
    load_sem, a_send_sem, a_recv_sem, y_send_sem, y_recv_sem, f_send_sem, f_recv_sem, fy_send_sem, fy_recv_sem,
    s_send_sem, s_recv_sem, z_send_sem, z_recv_sem, b_send_sem, b_recv_sem, g_send_sem, g_recv_sem,
    c_send_sem, c_recv_sem,
):
    R, C, K, piece, width, base, H, inv_root, scale = dims
    ow = width // H
    me_r = lax.axis_index("row")
    me_c = lax.axis_index("col")

    Y = C // 2
    core, me_y = lax.rem(me_c, 2), me_c // 2
    partner = me_y * 2 + (1 - core)

    flip = me_r // (R // 2)
    fr = me_r + flip * (R - 1 - 2 * me_r)
    is_owner = fr >= base
    mine_h = fr - base

    def unflip(row):
        return row + flip * (R - 1 - 2 * row)

    def block(k):
        if k == H - 1:
            near = jnp.maximum(mine_h, 0)
        else:
            near = (H - 1 - k) - (mine_h >= H - 1 - k).astype(jnp.int32)
        return unflip(base + near) - base

    def arrival(k):
        if k == 0:
            near = jnp.maximum(mine_h, 0)
        else:
            near = (k - 1) + (mine_h <= k - 1).astype(jnp.int32)
        return unflip(base + near) - base

    def listener(k):
        return unflip((R - 1 - k) - (fr >= R - 1 - k).astype(jnp.int32))

    def y_peer(k):
        return lax.rem(me_y + k, Y) * 2 + core

    def col_peer_of(k):
        return (1 - core) * Y + k if k < Y else core * Y + k - Y

    def row_peer(k):
        return lax.rem(me_r + k, R)

    def row_from(k):
        return lax.rem(me_r + (R - k), R)

    span = piece // SUB
    n_load = C * SUB

    def load(i):
        start = col_peer_of(i // SUB) * piece + (i % SUB) * span
        return pltpu.make_async_copy(
            slab_hbm.at[pl.ds(pl.multiple_of(start, span), span), :],
            slab.at[i // SUB, pl.ds((i % SUB) * span, span), :],
            load_sem.at[i],
        )

    seed_copy = pltpu.make_async_copy(seed_hbm, seed_ref, load_sem.at[n_load])
    sku_copy = pltpu.make_async_copy(sku_hbm, sku_ref, load_sem.at[n_load + 1])
    seed_copy.start()
    sku_copy.start()
    for i in range(min(DEPTH, n_load)):
        load(i).start()

    barrier = pltpu.get_barrier_semaphore()
    for k in range(1, R):
        pl.semaphore_signal(barrier, inc=1, device_id={"row": row_peer(k)}, device_id_type=MESH)
    for k in range(1, C):
        pl.semaphore_signal(barrier, inc=1, device_id={"col": lax.rem(me_c + k, C)}, device_id_type=MESH)

    seed_copy.wait()
    sku_copy.wait()
    index = lax.broadcasted_iota(jnp.int32, (K, width), 0)
    seeds = jnp.zeros((K, width), jnp.int32)
    for k in range(K):
        seeds = jnp.where(index == k, seed_ref[k], seeds)
    x_ref[...] = test_matrix(seeds, jnp.broadcast_to(sku_ref[...], (K, width)), width * C)

    def flip_task(i):
        here = slice((i % SUB) * span, (i % SUB + 1) * span)
        slab_t[i // SUB, :, here] = slab[i // SUB, here, :].T

    pending = []

    def col_copy(src, dst, send, recv, target):
        return pltpu.make_async_remote_copy(
            src_ref=src, dst_ref=dst, send_sem=send, recv_sem=recv,
            device_id={"col": lax.rem(target, C)}, device_id_type=MESH,
        )

    def row_copy(src, dst, send, recv, row):
        return pltpu.make_async_remote_copy(
            src_ref=src, dst_ref=dst, send_sem=send, recv_sem=recv,
            device_id={"row": row}, device_id_type=MESH,
        )

    def position(c):
        half = c // Y
        same = 1 - (half + core - 2 * half * core)
        return lax.rem(c, Y) + Y * same

    def half_copy(it, q):
        return col_copy(part.at[it, q], half_recv.at[it, q], a_send_sem.at[it, q], a_recv_sem.at[it, q], partner)

    def send_half(it, q):
        half_copy(it, q).start()
        pending.append(half_copy(it, q))

    def send_y(it, q, value):
        half_copy(it, q).wait_recv()
        y_sum[it, q, me_y] = value + half_recv[it, q]
        for k in range(1, Y):
            copy = col_copy(
                y_sum.at[it, q, me_y], y_sum.at[it, q, me_y],
                y_send_sem.at[it, q, k], y_recv_sem.at[it, q, k], y_peer(k),
            )
            copy.start()
            pending.append(copy)

    def square(value):
        return lax.dot_general(
            value, value, (((1,), (1,)), ((), ())), precision=HIGHEST, preferred_element_type=jnp.float32
        )

    def gram_copy(it, row, source):
        return row_copy(
            gsend_row.at[it], grecv_row.at[it, source], g_send_sem.at[it, row], g_recv_sem.at[it, source], row
        )

    def z_copy(it, h, source):
        return row_copy(
            zpart.at[it, h], zrecv.at[it, source], z_send_sem.at[it, h], z_recv_sem.at[it, source], base + h
        )

    def back_copy(it, row, h):
        return row_copy(
            back.at[it, h], back.at[it, h], b_send_sem.at[it, row], b_recv_sem.at[it, h], row
        )

    def gather_project(it):
        for k in range(H):
            h = arrival(k)
            if k == 0:
                @pl.when(jnp.logical_not(is_owner))
                def _():
                    back_copy(it, me_r, h).wait_recv()
            else:
                back_copy(it, me_r, h).wait_recv()
            rows = pl.ds(pl.multiple_of(h * ow, ow), ow)

            def product(slot, h=h, rows=rows):
                return jnp.dot(back[it, h], slab_t[slot, rows, :], preferred_element_type=jnp.float32)

            if k < H - 1:
                for slot in range(C):
                    value = product(slot)
                    acc[slot] = value if k == 0 else acc[slot] + value
        return lambda slot: acc[slot] + product(slot)

    for it in range(ITERS):
        if it == 0:
            for i in range(n_load):
                k, sub = i // SUB, i % SUB
                here = slice(sub * span, (sub + 1) * span)
                load(i).wait()
                if i + DEPTH < n_load:
                    load(i + DEPTH).start()
                value = lax.dot_general(
                    x_ref[...], slab[k, here, :], (((1,), (1,)), ((), ())), preferred_element_type=jnp.float32
                )
                if k < Y:
                    part[it, k, :, here] = value
                    if i == Y * SUB - 1:
                        pl.semaphore_wait(barrier, (R - 1) + (C - 1))
                        for q in range(Y):
                            send_half(it, q)
                else:
                    acc[k, :, here] = value
                    if sub == SUB - 1:
                        send_y(it, k - Y, acc[k])
        else:
            last = gather_project(it - 1)
            for q in range(Y):
                part[it, q] = last(q)
                send_half(it, q)
            for q in range(Y):
                value = last(Y + q)
                send_y(it, q, value)
        if it == 0:
            for i in TASKS[0]:
                flip_task(i)
        for q in range(C):
            at = Y + q if q < Y else q - Y
            if q < Y:
                c = core * Y + q
                for k in range(1, Y):
                    source = lax.rem(me_y + (Y - k), Y)
                    col_copy(
                        y_sum.at[it, q, source], y_sum.at[it, q, source],
                        y_send_sem.at[it, q, k], y_recv_sem.at[it, q, k], y_peer(k),
                    ).wait_recv()
                value = y_sum[it, q, 0]
                for y in range(1, Y):
                    value = value + y_sum[it, q, y]
                if it > 0:
                    value = value * inv_root
                s_ref[it, c] = value
                copy = col_copy(
                    s_ref.at[it, c], s_ref.at[it, c], s_send_sem.at[it, q], s_recv_sem.at[it, q], partner
                )
                copy.start()
                pending.append(copy)
            else:
                c = (1 - core) * Y + q - Y
                col_copy(
                    s_ref.at[it, c], s_ref.at[it, c], s_send_sem.at[it, q - Y], s_recv_sem.at[it, q - Y], partner
                ).wait_recv()
                value = s_ref[it, c]
            high = value.astype(jnp.bfloat16)
            low = (value - high.astype(jnp.float32)).astype(jnp.bfloat16)
            lhs[:K, :] = high
            lhs[K:, :] = low
            if q < C - 1 or ow % 128:
                product = jnp.dot(lhs[...], slab[at], preferred_element_type=jnp.float32)
                product = product[:K] + product[K:]
                zacc[...] = product if q == 0 else zacc[...] + product
            gram_part[it, c] = square(value)
        gram = gram_part[it, 0]
        for c in range(1, C):
            gram = gram + gram_part[it, c]

        gsend_row[it] = gram
        for k in range(H - 1):
            gram_copy(it, base + block(k), me_r).start()

        @pl.when(jnp.logical_not(is_owner))
        def _():
            gram_copy(it, base + block(H - 1), me_r).start()

        @pl.when(is_owner)
        def _():
            grecv_row[it, me_r] = gsend_row[it]

        if ow % 128:
            for h in range(H):
                zpart[it, h] = zacc[:, h * ow : (h + 1) * ow]
        for k in range(H):
            h = block(k)
            if ow % 128 == 0:
                cols = pl.ds(pl.multiple_of(h * ow, ow), ow)
                product = jnp.dot(lhs[...], slab[Y - 1, :, cols], preferred_element_type=jnp.float32)
                zpart[it, h] = zacc[:, cols] + product[:K] + product[K:]
            if k < H - 1:
                z_copy(it, h, me_r).start()
            else:
                @pl.when(jnp.logical_not(is_owner))
                def _():
                    z_copy(it, h, me_r).start()

        if it == 0:
            for i in TASKS[1]:
                flip_task(i)

        @pl.when(is_owner)
        def _():
            for k in range(1, R):
                gram_copy(it, me_r, row_from(k)).wait_recv()
            total = grecv_row[it, 0]
            for r in range(1, R):
                total = total + grecv_row[it, r]
            _, inverse = factorize(total)
            own = me_r - base
            total = zpart[it, own]
            for k in range(1, R):
                source = row_from(k)
                z_copy(it, own, source).wait_recv()
                total = total + zrecv[it, source]
            back[it, own] = jnp.dot(
                inverse, total, precision=HIGHEST, preferred_element_type=jnp.float32
            ).astype(jnp.bfloat16)
            for k in range(R - 1):
                back_copy(it, listener(k), own).start()

        if it == 0:
            for i in TASKS[2]:
                flip_task(i)

    last = gather_project(ITERS - 1)
    inner = []
    for y in range(Y):
        fin_part[y] = last(position(y * 2 + (1 - core)))
        copy = col_copy(fin_part.at[y], fin_recv.at[y], f_send_sem.at[y], f_recv_sem.at[y], partner)
        copy.start()
        inner.append(copy)
    for k in list(range(1, Y)) + [0]:
        y = lax.rem(me_y + k, Y)
        fin_sum[k] = last(position(y * 2 + core))
    for copy in inner:
        copy.wait_recv()
    pending += inner
    outer = []
    for k in range(1, Y):
        y = lax.rem(me_y + k, Y)
        fin_sum[k] = fin_sum[k] + fin_recv[y]
        copy = col_copy(fin_sum.at[k], fin_y.at[k], fy_send_sem.at[k], fy_recv_sem.at[k], y_peer(k))
        copy.start()
        outer.append(copy)
    own = fin_sum[0] + fin_recv[me_y]
    for k, copy in enumerate(outer):
        copy.wait_recv()
        own = own + fin_y[k + 1]
    pending += outer
    own = own * inv_root
    gcol[...] = square(own)
    copies = []
    for k in range(1, C):
        copy = col_copy(gcol, grecv_col.at[me_c], c_send_sem.at[k], c_recv_sem.at[k], me_c + k)
        copy.start()
        copies.append(copy)
    grecv_col[me_c] = gcol[...]
    for k in range(1, C):
        source = lax.rem(me_c + (C - k), C)
        col_copy(gcol, grecv_col.at[source], c_send_sem.at[k], c_recv_sem.at[k], me_c + k).wait_recv()
    pending += copies
    gram = grecv_col[0]
    for c in range(1, C):
        gram = gram + grecv_col[c]
    gsend_row[ITERS] = gram
    for k in list(range(R // 2, R)) + list(range(1, R // 2)):
        copy = gram_copy(ITERS, row_peer(k), me_r)
        copy.start()
        pending.append(copy)
    grecv_row[ITERS, me_r] = gram

    for copy in pending:
        copy.wait_send()
    for it in range(ITERS):
        for k in range(H - 1):
            gram_copy(it, base + block(k), me_r).wait_send()
            z_copy(it, block(k), me_r).wait_send()

        @pl.when(jnp.logical_not(is_owner))
        def _():
            gram_copy(it, base + block(H - 1), me_r).wait_send()
            z_copy(it, block(H - 1), me_r).wait_send()

        @pl.when(is_owner)
        def _():
            for k in range(R - 1):
                back_copy(it, listener(k), me_r - base).wait_send()

    for k in range(1, R):
        gram_copy(ITERS, me_r, row_from(k)).wait_recv()
    gram = grecv_row[ITERS, 0]
    for r in range(1, R):
        gram = gram + grecv_row[ITERS, r]
    upper, inverse = factorize(gram)
    ortho = jnp.dot(inverse, own, precision=HIGHEST, preferred_element_type=jnp.float32)
    basis_ref[...] = ortho * scale
    factor_ref[...] = upper / scale


def body(affinity, seed_values, sku_ids):
    R, C = lax.axis_size("row"), lax.axis_size("col")
    K = seed_values.shape[0]
    rows, width = affinity.shape
    piece, Y = rows // C, C // 2
    base, H = R // 4, R // 2
    ow = width // H
    dims = (R, C, K, piece, width, base, H, 1.0 / math.sqrt(width * C), math.sqrt(rows * R))
    f32, bf16 = jnp.float32, jnp.bfloat16
    dma = pltpu.SemaphoreType.DMA
    vmem = pl.BlockSpec(memory_space=pltpu.VMEM)
    return pl.pallas_call(
        functools.partial(kernel, dims),
        out_shape=(
            jax.ShapeDtypeStruct((K, piece), f32),
            jax.ShapeDtypeStruct((K, K), f32),
        ),
        in_specs=[pl.BlockSpec(memory_space=pl.ANY)] * 3,
        out_specs=(vmem, vmem),
        scratch_shapes=[
            pltpu.VMEM((C, piece, width), bf16),
            pltpu.VMEM((C, width, piece), bf16),
            pltpu.SMEM((K,), jnp.int32),
            pltpu.VMEM((1, width), jnp.int32),
            pltpu.VMEM((K, width), bf16),
            pltpu.VMEM((C, K, piece), f32),
            pltpu.VMEM((ITERS, Y, K, piece), f32),
            pltpu.VMEM((ITERS, Y, K, piece), f32),
            pltpu.VMEM((ITERS, Y, Y, K, piece), f32),
            pltpu.VMEM((Y, K, piece), f32),
            pltpu.VMEM((Y, K, piece), f32),
            pltpu.VMEM((Y, K, piece), f32),
            pltpu.VMEM((Y, K, piece), f32),
            pltpu.VMEM((ITERS, C, K, piece), f32),
            pltpu.VMEM((2 * K, piece), bf16),
            pltpu.VMEM((K, width), f32),
            pltpu.VMEM((ITERS, H, K, ow), f32),
            pltpu.VMEM((ITERS, R, K, ow), f32),
            pltpu.VMEM((ITERS, H, K, ow), bf16),
            pltpu.VMEM((ITERS + 1, K, K), f32),
            pltpu.VMEM((ITERS + 1, R, K, K), f32),
            pltpu.VMEM((C, K, K), f32),
            pltpu.VMEM((K, K), f32),
            pltpu.VMEM((ITERS, C, K, K), f32),
            dma((C * SUB + 2,)),
            dma((ITERS, Y)), dma((ITERS, Y)),
            dma((ITERS, Y, Y)), dma((ITERS, Y, Y)),
            dma((Y,)), dma((Y,)),
            dma((Y,)), dma((Y,)),
            dma((ITERS, Y)), dma((ITERS, Y)),
            dma((ITERS, H)), dma((ITERS, R)),
            dma((ITERS, R)), dma((ITERS, H)),
            dma((ITERS + 1, R)), dma((ITERS + 1, R)),
            dma((C,)), dma((C,)),
        ],
        compiler_params=pltpu.CompilerParams(
            collective_id=0, has_side_effects=True, vmem_limit_bytes=60 * 1024 * 1024
        ),
    )(affinity, seed_values, sku_ids[None, :])


def solution(mesh):
    placed = (P("row", "col"), P(), P("col"))
    return jax.shard_map(
        body, mesh=mesh, in_specs=placed, out_specs=(P(None, ("row", "col")), P()), check_vma=False
    )
```

time: 66.6 us -> 64.8 us (0.973)
  Pallas kernels: 62.9 us -> 61.2 us
    pallas_call x1, Pallas kernels: 62.9 us -> 61.2 us  [body(): pl.pallas_call(functools.partial(kernel, dims), out_shape=(jax.ShapeDtype...]
where the time goes in v1:
time: 64.8 us; the launch traced here: 64.6 us
  Pallas kernels  61.2 us (94%)
  local copies, waits for them, and re-layouts  2.77 us (4%)
    pallas_call x1, Pallas kernels, body(): pl.pallas_call(functools.partial(kernel, dims), out_shape=(jax.ShapeDtype...  61.2 us
    unnamed x2, local copies, waits for them, and re-layouts  2.77 us

profile of v1, /device:TPU:0, one launch (start us, length us, event | category | flops | bytes accessed | tf_op | source)
XLA Modules:
  0.0 64.6 jit_solution(8795530587355987076)
XLA Ops:
  0.6 61.2 %shard_map.50 = (f32[16,1024]{1,0:T(8,128)}, f32[16,16]{1,0:T(8,128)}) custom-call(bf16[4096,2048]{1,0:T(8,128)(2,1)} %slab_hbm.1, s32[16]{0:T(128)} %seed_hbm.1, s32[1,2048]{1,0:T(1,128)} %bitcast.1), custom_call_target="tpu_custom_call" | custom-call | tf_op jit(solution)/shard_map/pallas_call | solution.py:447
  61.8 1.5 %copy.7 = f32[16,1024]{1,0:T(8,128)} copy(f32[16,1024]{1,0:T(8,128)} %get-tuple-element.4) | data formatting | bytes 131072
  63.3 1.3 %copy.8 = f32[16,16]{1,0:T(8,128)} copy(f32[16,16]{1,0:T(8,128)} %get-tuple-element.5) | data formatting | bytes 2048

commit v2 on v1

v2 whole, which is shorter than its diff:
```python
import functools
import math

import jax
import jax.numpy as jnp
from jax import lax
from jax.experimental import pallas as pl
from jax.experimental.pallas import tpu as pltpu
from jax.sharding import PartitionSpec as P

ITERS = 2
SUB = 2
DEPTH = 4
LANES = 128
TASKS = ((0, 1), (2, 3, 4), (5, 6, 7))
HIGHEST = lax.Precision.HIGHEST
MESH = pl.DeviceIdType.MESH

mix_first = -2048144789
mix_second = -1028477387
golden = -1640531535
salt_value = 1540483477


def shifted(value, amount):
    return lax.shift_right_logical(value, jnp.full(value.shape, amount, jnp.int32))


def scramble(value):
    value = jnp.bitwise_xor(value, shifted(value, 16))
    value = value * jnp.int32(mix_first)
    value = jnp.bitwise_xor(value, shifted(value, 13))
    value = value * jnp.int32(mix_second)
    return jnp.bitwise_xor(value, shifted(value, 16))


def test_matrix(seeds, skus, total_columns):
    first = scramble(jnp.bitwise_xor(seeds, skus * jnp.int32(golden)))
    second = scramble(jnp.bitwise_xor(first, jnp.int32(salt_value)))
    uniform_a = (shifted(first, 9) + 1).astype(jnp.float32) / 8388608.0
    uniform_b = (shifted(second, 9) + 1).astype(jnp.float32) / 8388608.0
    gauss = jnp.sqrt(-2.0 * jnp.log(uniform_a)) * jnp.cos(6.283185307179586 * uniform_b)
    return (gauss / math.sqrt(total_columns)).astype(jnp.bfloat16)


def factorize(gram):
    count = gram.shape[0]
    rows = lax.broadcasted_iota(jnp.int32, (count, count), 0)
    cols = lax.broadcasted_iota(jnp.int32, (count, count), 1)
    left = gram
    right = (rows == cols).astype(jnp.float32)
    for j in range(count):
        pivot = left[j : j + 1, j : j + 1]
        inv = lax.rsqrt(pivot)
        inv = inv * (1.5 - 0.5 * (pivot * inv) * inv)
        left_row = left[j : j + 1, :] * inv
        right_row = right[j : j + 1, :] * inv
        factor = left[:, j : j + 1] * inv
        left = jnp.where(rows == j, left_row, jnp.where(rows > j, left - factor * left_row, left))
        right = jnp.where(rows == j, right_row, jnp.where(rows > j, right - factor * right_row, right))
    return jnp.where(rows <= cols, left, 0.0), right


def repeat(start, stop, step):
    if stop - start <= 64:
        for k in range(start, stop):
            step(k)
    else:
        lax.fori_loop(start, stop, lambda k, _: (step(k), 0)[1], 0)


def kernel(
    dims,
    slab_hbm, seed_hbm, sku_hbm,
    basis_ref, factor_ref,
    slab, slab_t, seed_ref, sku_ref, x_ref, acc, part, half_recv, y_send, y_sum,
    fin_part, fin_recv, fin_send, fin_y, s_ref, lhs, zacc, zpart, zrecv, block_ref, back,
    gsend, grecv, fsend, frecv,
    load_sem, a_send_sem, a_recv_sem, y_send_sem, y_recv_sem, f_send_sem, f_recv_sem, fy_send_sem, fy_recv_sem,
    s_send_sem, s_recv_sem, z_send_sem, z_recv_sem, b_send_sem, b_recv_sem, g_send_sem, g_recv_sem,
    c_send_sem, c_recv_sem,
):
    R, C, K, piece, width, base, H, W, inv_root, scale = dims
    wave = width // W
    bw = wave // H
    me_r = lax.axis_index("row")
    me_c = lax.axis_index("col")
    me = me_r * C + me_c

    Y = C // 2
    core, me_y = lax.rem(me_c, 2), me_c // 2
    other = 1 - core
    partner = me_y * 2 + other

    flip = me_r // (R // 2)
    is_owner = jnp.logical_and(me_r >= base, me_r < base + H)

    def far(k):
        return (H - 1 - k) + flip * (2 * k - H + 1)

    def far_row(k):
        return (R - 1 - k) + flip * (2 * k - R + 1)

    span = piece // SUB
    n_load = C * SUB

    def load(i):
        k = i // SUB
        start = ((other * Y + k) if k < Y else (core * Y + k - Y)) * piece + (i % SUB) * span
        return pltpu.make_async_copy(
            slab_hbm.at[pl.ds(pl.multiple_of(start, span), span), :],
            slab.at[k, pl.ds((i % SUB) * span, span), :],
            load_sem.at[i],
        )

    seed_copy = pltpu.make_async_copy(seed_hbm, seed_ref, load_sem.at[n_load])
    sku_copy = pltpu.make_async_copy(sku_hbm, sku_ref, load_sem.at[n_load + 1])
    seed_copy.start()
    sku_copy.start()
    for i in range(min(DEPTH, n_load)):
        load(i).start()

    def peer(k):
        index = lax.rem(me + k, R * C)
        return {"row": index // C, "col": lax.rem(index, C)}

    barrier = pltpu.get_barrier_semaphore()

    def greet(k):
        pl.semaphore_signal(barrier, inc=1, device_id=peer(k), device_id_type=MESH)

    repeat(1, R * C, greet)

    seed_copy.wait()
    sku_copy.wait()
    index = lax.broadcasted_iota(jnp.int32, (K, width), 0)
    seeds = jnp.zeros((K, width), jnp.int32)
    for k in range(K):
        seeds = jnp.where(index == k, seed_ref[k], seeds)
    x_ref[...] = test_matrix(seeds, jnp.broadcast_to(sku_ref[...], (K, width)), width * C)

    def turn(i):
        here = slice((i % SUB) * span, (i % SUB + 1) * span)
        slab_t[i // SUB, :, here] = slab[i // SUB, here, :].T

    pending = []

    def remote(src, dst, send, recv, row, col):
        return pltpu.make_async_remote_copy(
            src_ref=src, dst_ref=dst, send_sem=send, recv_sem=recv,
            device_id={"row": row, "col": col}, device_id_type=MESH,
        )

    def go(copy):
        copy.start()
        pending.append(copy)

    def position(c):
        half = c // Y
        same = 1 - (half + core - 2 * half * core)
        return lax.rem(c, Y) + Y * same

    def swap(it, slot):
        there = (slot + Y) % C
        return remote(
            part.at[it, slot], half_recv.at[it, there], a_send_sem.at[it, slot], a_recv_sem.at[it, there],
            me_r, partner,
        )

    def swapped(it, slot):
        return remote(
            part.at[it, slot], half_recv.at[it, slot], a_send_sem.at[it, slot], a_recv_sem.at[it, slot],
            me_r, partner,
        )

    def cross(it, q, k):
        y = lax.rem(me_y + k, Y)
        return remote(
            y_send.at[it, q], y_sum.at[it, q, me_y], y_send_sem.at[it, q, k], y_recv_sem.at[it, q, me_y],
            me_r, y * 2 + other,
        )

    def crossed(it, q, y):
        return remote(
            y_send.at[it, q], y_sum.at[it, q, y], y_send_sem.at[it, q, 0], y_recv_sem.at[it, q, y], me_r, partner
        )

    def square(value):
        return lax.dot_general(
            value, value, (((1,), (1,)), ((), ())), precision=HIGHEST, preferred_element_type=jnp.float32
        )

    def gram_copy(it, h, c, source):
        return remote(
            gsend.at[it], grecv.at[it, source], g_send_sem.at[it, h, c], g_recv_sem.at[it, source],
            base + h, me_y * 2 + c,
        )

    def z_copy(it, w, h, source):
        return remote(
            zpart.at[it, w, h], zrecv.at[it, w, source], z_send_sem.at[it, w, h], z_recv_sem.at[it, w, source],
            base + h, partner,
        )

    def back_copy(it, w, row, h):
        cols = pl.ds(pl.multiple_of(h * bw, bw), bw)
        return remote(
            block_ref.at[it, w], back.at[it, w, :, cols], b_send_sem.at[it, w, row], b_recv_sem.at[it, w, h],
            row, partner,
        )

    def gathered(it):
        def product(w, slot):
            rows = slice(w * wave, (w + 1) * wave)
            return jnp.dot(back[it, w], slab_t[slot, rows, :], preferred_element_type=jnp.float32)

        for w in range(W):
            for h in range(H):
                back_copy(it, w, me_r, h).wait_recv()
            if w < W - 1:
                for slot in range(C):
                    value = product(w, slot)
                    acc[slot] = value if w == 0 else acc[slot] + value
        if W == 1:
            return lambda slot: product(0, slot)
        return lambda slot: acc[slot] + product(W - 1, slot)

    for it in range(ITERS):
        def hand_over(q):
            swapped(it, Y + q).wait_recv()
            y_send[it, q] = part[it, Y + q] + half_recv[it, Y + q]
            for k in range(1, Y):
                go(cross(it, q, k))

        if it == 0:
            for i in range(n_load):
                k, sub = i // SUB, i % SUB
                here = slice(sub * span, (sub + 1) * span)
                load(i).wait()
                if i + DEPTH < n_load:
                    load(i + DEPTH).start()
                part[it, k, :, here] = lax.dot_general(
                    x_ref[...], slab[k, here, :], (((1,), (1,)), ((), ())), preferred_element_type=jnp.float32
                )
                if i == Y * SUB - 1:
                    pl.semaphore_wait(barrier, R * C - 1)
                    for slot in range(Y):
                        go(swap(it, slot))
                if k >= Y and sub == SUB - 1:
                    go(swap(it, k))
                    hand_over(k - Y)
            for i in TASKS[0]:
                turn(i)
        else:
            last = gathered(it - 1)
            for slot in range(C):
                part[it, slot] = last(slot)
                go(swap(it, slot))
            for q in range(Y):
                hand_over(q)
        for q in range(Y):
            swapped(it, q).wait_recv()
            y_sum[it, q, me_y] = part[it, q] + half_recv[it, q]

        gram = None
        for slot in range(C):
            if slot < Y:
                for k in range(1, Y):
                    crossed(it, slot, lax.rem(me_y + (Y - k), Y)).wait_recv()
                value = y_sum[it, slot, 0]
                for y in range(1, Y):
                    value = value + y_sum[it, slot, y]
                if it > 0:
                    value = value * inv_root
                s_ref[it, slot] = value
                go(
                    remote(
                        s_ref.at[it, slot], s_ref.at[it, Y + slot], s_send_sem.at[it, slot], s_recv_sem.at[it, slot],
                        me_r, partner,
                    )
                )
                gram = square(value) if slot == 0 else gram + square(value)
                if slot == Y - 1:
                    gsend[it] = gram
                    for k in range(H):
                        h = far(k)
                        go(gram_copy(it, h, other, me_r * 2 + core))

                        @pl.when(me_r != base + h)
                        def _():
                            gram_copy(it, h, core, me_r * 2 + core).start()

                    @pl.when(is_owner)
                    def _():
                        grecv[it, me_r * 2 + core] = gsend[it]
            else:
                remote(
                    s_ref.at[it, slot - Y], s_ref.at[it, slot],
                    s_send_sem.at[it, slot - Y], s_recv_sem.at[it, slot - Y], me_r, partner,
                ).wait_recv()
                value = s_ref[it, slot]
            high = value.astype(jnp.bfloat16)
            low = (value - high.astype(jnp.float32)).astype(jnp.bfloat16)
            lhs[:K, :] = high
            lhs[K:, :] = low
            if slot < C - 1:
                product = jnp.dot(lhs[...], slab[slot], preferred_element_type=jnp.float32)
                product = product[:K] + product[K:]
                zacc[...] = product if slot == 0 else zacc[...] + product
        for w in range(W):
            cols = slice(w * wave, (w + 1) * wave)
            product = jnp.dot(lhs[...], slab[C - 1, :, cols], preferred_element_type=jnp.float32)
            product = zacc[:, cols] + product[:K] + product[K:]
            for h in range(H):
                zpart[it, w, h] = product[:, h * bw : (h + 1) * bw]
            for k in range(H):
                go(z_copy(it, w, far(k), me_r))

        if it == 0:
            for i in TASKS[1]:
                turn(i)

        @pl.when(is_owner)
        def _():
            gram_copy(it, me_r - base, core, me_r * 2 + other).wait_recv()
            for k in range(1, R):
                source = lax.rem(me_r + k, R) * 2
                gram_copy(it, me_r - base, core, source).wait_recv()
                gram_copy(it, me_r - base, core, source + 1).wait_recv()
            total = grecv[it, 0]
            for r in range(1, 2 * R):
                total = total + grecv[it, r]
            _, inverse = factorize(total)
            own = me_r - base
            for w in range(W):
                for r in range(R):
                    z_copy(it, w, own, r).wait_recv()
                total = zrecv[it, w, 0]
                for r in range(1, R):
                    total = total + zrecv[it, w, r]
                block_ref[it, w] = jnp.dot(
                    inverse, total, precision=HIGHEST, preferred_element_type=jnp.float32
                ).astype(jnp.bfloat16)
                for k in range(R):
                    back_copy(it, w, far_row(k), own).start()

        if it == 0:
            for i in TASKS[2]:
                turn(i)

    last = gathered(ITERS - 1)

    def to_partner(k):
        y = lax.rem(me_y + k, Y)
        return remote(
            fin_part.at[k], fin_recv.at[k], f_send_sem.at[k], f_recv_sem.at[k], me_r, partner
        ), y

    for k in list(range(1, Y)) + [0]:
        copy, y = to_partner(k)
        fin_part[k] = last(position(y * 2 + (core if k else other)))
        go(copy)
    for k in list(range(1, Y)) + [0]:
        y = lax.rem(me_y + k, Y)
        fin_send[k] = last(position(y * 2 + (other if k else core)))
    outer = []
    for k in range(1, Y):
        copy, y = to_partner(k)
        copy.wait_recv()
        fin_send[k] = fin_send[k] + fin_recv[k]
        copy = remote(
            fin_send.at[k], fin_y.at[k], fy_send_sem.at[k], fy_recv_sem.at[k], me_r, y * 2 + other
        )
        go(copy)
        outer.append(copy)
    to_partner(0)[0].wait_recv()
    own = fin_send[0] + fin_recv[0]
    for k, copy in enumerate(outer):
        copy.wait_recv()
        own = own + fin_y[k + 1]
    own = own * inv_root
    fsend[...] = square(own)

    def spread(k):
        return pltpu.make_async_remote_copy(
            src_ref=fsend, dst_ref=frecv.at[me], send_sem=c_send_sem.at[k],
            recv_sem=c_recv_sem.at[me], device_id=peer(k), device_id_type=MESH,
        )

    def collect(k):
        source = lax.rem(me + k, R * C)
        pltpu.make_async_remote_copy(
            src_ref=fsend, dst_ref=frecv.at[source], send_sem=c_send_sem.at[k],
            recv_sem=c_recv_sem.at[source], device_id=peer(k), device_id_type=MESH,
        ).wait_recv()

    repeat(1, R * C, lambda k: spread(k).start())
    frecv[me] = fsend[...]

    for copy in pending:
        copy.wait_send()
    for it in range(ITERS):
        for h in range(H):
            @pl.when(me_r != base + h)
            def _():
                gram_copy(it, h, core, me_r * 2 + core).wait_send()

        @pl.when(is_owner)
        def _():
            for w in range(W):
                for row in range(R):
                    back_copy(it, w, row, me_r - base).wait_send()

    repeat(1, R * C, collect)
    parts = [frecv[r] for r in range(8)]
    for r in range(8, R * C):
        parts[r % 8] = parts[r % 8] + frecv[r]
    while len(parts) > 1:
        parts = [a + b for a, b in zip(parts[::2], parts[1::2])]
    upper, inverse = factorize(parts[0])
    ortho = jnp.dot(inverse, own, precision=HIGHEST, preferred_element_type=jnp.float32)
    basis_ref[...] = ortho * scale
    factor_ref[...] = upper / scale
    repeat(1, R * C, lambda k: spread(k).wait_send())


def body(affinity, seed_values, sku_ids):
    R, C = lax.axis_size("row"), lax.axis_size("col")
    K = seed_values.shape[0]
    rows, width = affinity.shape
    piece, Y = rows // C, C // 2
    H = min(R // 2, width // LANES)
    W = 2 if width % (2 * H * LANES) == 0 else 1
    base, wave, bw = (R - H) // 2, width // W, width // W // H
    dims = (R, C, K, piece, width, base, H, W, 1.0 / math.sqrt(width * C), math.sqrt(rows * R))
    f32, bf16 = jnp.float32, jnp.bfloat16
    dma = pltpu.SemaphoreType.DMA
    vmem = pl.BlockSpec(memory_space=pltpu.VMEM)
    return pl.pallas_call(
        functools.partial(kernel, dims),
        out_shape=(
            jax.ShapeDtypeStruct((K, piece), f32),
            jax.ShapeDtypeStruct((K, K), f32),
        ),
        in_specs=[pl.BlockSpec(memory_space=pl.ANY)] * 3,
        out_specs=(vmem, vmem),
        scratch_shapes=[
            pltpu.VMEM((C, piece, width), bf16),
            pltpu.VMEM((C, width, piece), bf16),
            pltpu.SMEM((K,), jnp.int32),
            pltpu.VMEM((1, width), jnp.int32),
            pltpu.VMEM((K, width), bf16),
            pltpu.VMEM((C, K, piece), f32),
            pltpu.VMEM((ITERS, C, K, piece), f32),
            pltpu.VMEM((ITERS, C, K, piece), f32),
            pltpu.VMEM((ITERS, Y, K, piece), f32),
            pltpu.VMEM((ITERS, Y, Y, K, piece), f32),
            pltpu.VMEM((Y, K, piece), f32),
            pltpu.VMEM((Y, K, piece), f32),
            pltpu.VMEM((Y, K, piece), f32),
            pltpu.VMEM((Y, K, piece), f32),
            pltpu.VMEM((ITERS, C, K, piece), f32),
            pltpu.VMEM((2 * K, piece), bf16),
            pltpu.VMEM((K, width), f32),
            pltpu.VMEM((ITERS, W, H, K, bw), f32),
            pltpu.VMEM((ITERS, W, R, K, bw), f32),
            pltpu.VMEM((ITERS, W, K, bw), bf16),
            pltpu.VMEM((ITERS, W, K, wave), bf16),
            pltpu.VMEM((ITERS, K, K), f32),
            pltpu.VMEM((ITERS, 2 * R, K, K), f32),
            pltpu.VMEM((K, K), f32),
            pltpu.VMEM((R * C, K, K), f32),
            dma((C * SUB + 2,)),
            dma((ITERS, C)), dma((ITERS, C)),
            dma((ITERS, Y, Y)), dma((ITERS, Y, Y)),
            dma((Y,)), dma((Y,)),
            dma((Y,)), dma((Y,)),
            dma((ITERS, Y)), dma((ITERS, Y)),
            dma((ITERS, W, H)), dma((ITERS, W, R)),
            dma((ITERS, W, R)), dma((ITERS, W, H)),
            dma((ITERS, H, 2)), dma((ITERS, 2 * R)),
            dma((R * C,)), dma((R * C,)),
        ],
        compiler_params=pltpu.CompilerParams(
            collective_id=0, has_side_effects=True, vmem_limit_bytes=60 * 1024 * 1024
        ),
    )(affinity, seed_values, sku_ids[None, :])


def solution(mesh):
    placed = (P("row", "col"), P(), P("col"))
    return jax.shard_map(
        body, mesh=mesh, in_specs=placed, out_specs=(P(None, ("row", "col")), P()), check_vma=False
    )
```

time: 64.8 us -> 61.2 us (0.944)
  the two profiles are of different devices: /device:TPU:0 before, /device:TPU:15 now
where the time goes in v2:
time: 61.2 us; the launch traced here: 61 us
  Pallas kernels  57.6 us (94%)
  local copies, waits for them, and re-layouts  2.77 us (5%)
  between operations  0.64 us (1%)
    pallas_call x1, Pallas kernels, body(): pl.pallas_call(functools.partial(kernel, dims), out_shape=(jax.ShapeDtype...  57.6 us
    unnamed x2, local copies, waits for them, and re-layouts  2.77 us

profile of v2, /device:TPU:15, one launch (start us, length us, event | category | flops | bytes accessed | tf_op | source)
XLA Modules:
  0.0 61.0 jit_solution(11715226446821610394)
XLA Ops:
  0.6 57.6 %shard_map.50 = (f32[16,1024]{1,0:T(8,128)}, f32[16,16]{1,0:T(8,128)}) custom-call(bf16[4096,2048]{1,0:T(8,128)(2,1)} %slab_hbm.1, s32[16]{0:T(128)} %seed_hbm.1, s32[1,2048]{1,0:T(1,128)} %bitcast.1), custom_call_target="tpu_custom_call" | custom-call | tf_op jit(solution)/shard_map/pallas_call | solution.py:439
  58.3 1.5 %copy.7 = f32[16,1024]{1,0:T(8,128)} copy(f32[16,1024]{1,0:T(8,128)} %get-tuple-element.4) | data formatting | bytes 131072
  59.7 1.3 %copy.8 = f32[16,16]{1,0:T(8,128)} copy(f32[16,16]{1,0:T(8,128)} %get-tuple-element.5) | data formatting | bytes 2048

commit v3 on v2

v3 whole, which is shorter than its diff:
```python
import functools
import math

import jax
import jax.numpy as jnp
from jax import lax
from jax.experimental import pallas as pl
from jax.experimental.pallas import tpu as pltpu
from jax.sharding import PartitionSpec as P

ITERS = 2
SUB = 2
DEPTH = 4
LANES = 128
TASKS = ((0, 1), (2, 3, 4), (5,), (6, 7))
HIGHEST = lax.Precision.HIGHEST
MESH = pl.DeviceIdType.MESH

mix_first = -2048144789
mix_second = -1028477387
golden = -1640531535
salt_value = 1540483477


def shifted(value, amount):
    return lax.shift_right_logical(value, jnp.full(value.shape, amount, jnp.int32))


def scramble(value):
    value = jnp.bitwise_xor(value, shifted(value, 16))
    value = value * jnp.int32(mix_first)
    value = jnp.bitwise_xor(value, shifted(value, 13))
    value = value * jnp.int32(mix_second)
    return jnp.bitwise_xor(value, shifted(value, 16))


def test_matrix(seeds, skus, total_columns):
    first = scramble(jnp.bitwise_xor(seeds, skus * jnp.int32(golden)))
    second = scramble(jnp.bitwise_xor(first, jnp.int32(salt_value)))
    uniform_a = (shifted(first, 9) + 1).astype(jnp.float32) / 8388608.0
    uniform_b = (shifted(second, 9) + 1).astype(jnp.float32) / 8388608.0
    gauss = jnp.sqrt(-2.0 * jnp.log(uniform_a)) * jnp.cos(6.283185307179586 * uniform_b)
    return (gauss / math.sqrt(total_columns)).astype(jnp.bfloat16)


def factorize(gram):
    count = gram.shape[0]
    rows = lax.broadcasted_iota(jnp.int32, (count, count), 0)
    cols = lax.broadcasted_iota(jnp.int32, (count, count), 1)
    left = gram
    right = (rows == cols).astype(jnp.float32)
    for j in range(count):
        pivot = left[j : j + 1, j : j + 1]
        inv = lax.rsqrt(pivot)
        inv = inv * (1.5 - 0.5 * (pivot * inv) * inv)
        left_row = left[j : j + 1, :] * inv
        right_row = right[j : j + 1, :] * inv
        factor = left[:, j : j + 1] * inv
        left = jnp.where(rows == j, left_row, jnp.where(rows > j, left - factor * left_row, left))
        right = jnp.where(rows == j, right_row, jnp.where(rows > j, right - factor * right_row, right))
    return jnp.where(rows <= cols, left, 0.0), right


def repeat(start, stop, step):
    if stop - start <= 64:
        for k in range(start, stop):
            step(k)
    else:
        lax.fori_loop(start, stop, lambda k, _: (step(k), 0)[1], 0)


def kernel(
    dims,
    slab_hbm, seed_hbm, sku_hbm,
    basis_ref, factor_ref,
    slab, slab_t, seed_ref, sku_ref, x_ref, acc, part, half_recv, y_send, y_sum,
    fin_part, fin_recv, fin_send, fin_y, s_ref, lhs, zacc, zpart, zrecv, block_ref, back,
    gsend, grecv, fsend, frecv,
    load_sem, send_sem, a_recv_sem, y_recv_sem, f_recv_sem, fy_recv_sem, s_recv_sem, z_recv_sem, b_recv_sem,
    g_recv_sem, c_recv_sem,
):
    R, C, K, piece, width, base, H, W, inv_root, scale = dims
    wave = width // W
    bw = wave // H
    me_r = lax.axis_index("row")
    me_c = lax.axis_index("col")
    me = me_r * C + me_c

    Y = C // 2
    core, me_y = lax.rem(me_c, 2), me_c // 2
    other = 1 - core
    partner = me_y * 2 + other

    flip = me_r // (R // 2)
    is_owner = jnp.logical_and(me_r >= base, me_r < base + H)

    def far(k):
        return (H - 1 - k) + flip * (2 * k - H + 1)

    def far_row(k):
        return (R - 1 - k) + flip * (2 * k - R + 1)

    span = piece // SUB
    n_load = C * SUB

    def load(i):
        k = i // SUB
        start = ((other * Y + k) if k < Y else (core * Y + k - Y)) * piece + (i % SUB) * span
        return pltpu.make_async_copy(
            slab_hbm.at[pl.ds(pl.multiple_of(start, span), span), :],
            slab.at[pl.ds(i * span, span), :],
            load_sem.at[i % DEPTH],
        )

    seed_copy = pltpu.make_async_copy(seed_hbm, seed_ref, load_sem.at[DEPTH])
    sku_copy = pltpu.make_async_copy(sku_hbm, sku_ref, load_sem.at[DEPTH + 1])
    seed_copy.start()
    sku_copy.start()
    for i in range(min(DEPTH, n_load)):
        load(i).start()

    def peer(k):
        index = lax.rem(me + k, R * C)
        return {"row": index // C, "col": lax.rem(index, C)}

    barrier = pltpu.get_barrier_semaphore()

    def greet(k):
        pl.semaphore_signal(barrier, inc=1, device_id=peer(k), device_id_type=MESH)

    repeat(1, R * C, greet)

    seed_copy.wait()
    sku_copy.wait()
    index = lax.broadcasted_iota(jnp.int32, (K, width), 0)
    seeds = jnp.zeros((K, width), jnp.int32)
    for k in range(K):
        seeds = jnp.where(index == k, seed_ref[k], seeds)
    x_ref[...] = test_matrix(seeds, jnp.broadcast_to(sku_ref[...], (K, width)), width * C)

    def turn(i):
        here = slice((i % SUB) * span, (i % SUB + 1) * span)
        slab_t[i // SUB, :, here] = slab[i * span : (i + 1) * span, :].T

    BULK, GRAM, OWN_GRAM, BLOCK, LAST_GRAM = range(5)

    def remote(kind, src, dst, recv, row, col):
        return pltpu.make_async_remote_copy(
            src_ref=src, dst_ref=dst, send_sem=send_sem.at[kind], recv_sem=recv,
            device_id={"row": row, "col": col}, device_id_type=MESH,
        )

    def sent(kind, ref):
        remote(kind, ref, ref, send_sem.at[kind], me_r, partner).wait_send()

    def sent_rows(kind, values, itemsize):
        sent(kind, slab.at[pl.ds(0, values * itemsize // (2 * width)), :])

    def position(c):
        half = c // Y
        same = 1 - (half + core - 2 * half * core)
        return lax.rem(c, Y) + Y * same

    def swap(it, slot):
        there = (slot + Y) % C
        return remote(BULK, part.at[it, slot], half_recv.at[it, there], a_recv_sem.at[it, there], me_r, partner)

    def swapped(it, slot):
        return remote(BULK, part.at[it, slot], half_recv.at[it, slot], a_recv_sem.at[it, slot], me_r, partner)

    def cross(it, q, k):
        y = lax.rem(me_y + k, Y)
        return remote(
            BULK, y_send.at[it, q], y_sum.at[it, q, me_y], y_recv_sem.at[it, q, k - 1], me_r, y * 2 + other
        )

    def crossed(it, q, k):
        y = lax.rem(me_y + (Y - k), Y)
        return remote(BULK, y_send.at[it, q], y_sum.at[it, q, y], y_recv_sem.at[it, q, k - 1], me_r, partner)

    def square(value):
        return lax.dot_general(
            value, value, (((1,), (1,)), ((), ())), precision=HIGHEST, preferred_element_type=jnp.float32
        )

    def gram_copy(it, h, c):
        slot = lax.rem(me_r * 2 + core - (base + h) * 2 - c - 1 + 4 * R, 2 * R)
        return remote(
            OWN_GRAM if c is core else GRAM, gsend.at[it], grecv.at[it, slot], g_recv_sem.at[it],
            base + h, me_y * 2 + c,
        )

    def z_copy(it, w, h):
        return remote(BULK, zpart.at[it, w, h], zrecv.at[it, w, me_r], z_recv_sem.at[it, w], base + h, partner)

    def back_copy(it, w, row, h):
        cols = pl.ds(pl.multiple_of(h * bw, bw), bw)
        return remote(BLOCK, block_ref.at[it, w], back.at[it, w, :, cols], b_recv_sem.at[it, w], row, partner)

    def landed(ref, sem):
        remote(BULK, ref, ref, sem, me_r, partner).wait_recv()

    def gathered(it):
        def product(w, slot):
            rows = slice(w * wave, (w + 1) * wave)
            return jnp.dot(back[it, w], slab_t[slot, rows, :], preferred_element_type=jnp.float32)

        for w in range(W):
            landed(back.at[it, w], b_recv_sem.at[it, w])
            if w < W - 1:
                for slot in range(C):
                    value = product(w, slot)
                    acc[slot] = value if w == 0 else acc[slot] + value
        if W == 1:
            return lambda slot: product(0, slot)
        return lambda slot: acc[slot] + product(W - 1, slot)

    for it in range(ITERS):
        def hand_over(q):
            swapped(it, Y + q).wait_recv()
            y_send[it, q] = part[it, Y + q] + half_recv[it, Y + q]
            for k in range(1, Y):
                cross(it, q, k).start()

        if it == 0:
            for i in range(n_load):
                k, sub = i // SUB, i % SUB
                here = slice(sub * span, (sub + 1) * span)
                load(i).wait()
                if i + DEPTH < n_load:
                    load(i + DEPTH).start()
                part[it, k, :, here] = lax.dot_general(
                    x_ref[...], slab[i * span : (i + 1) * span, :], (((1,), (1,)), ((), ())), preferred_element_type=jnp.float32
                )
                if i == Y * SUB - 1:
                    pl.semaphore_wait(barrier, R * C - 1)
                    for slot in range(Y):
                        swap(it, slot).start()
                if k >= Y and sub == SUB - 1:
                    swap(it, k).start()
                    hand_over(k - Y)
            for i in TASKS[0]:
                turn(i)
        else:
            last = gathered(it - 1)
            for slot in range(C):
                part[it, slot] = last(slot)
                swap(it, slot).start()
            for q in range(Y):
                hand_over(q)
        for q in range(Y):
            swapped(it, q).wait_recv()
            y_sum[it, q, me_y] = part[it, q] + half_recv[it, q]

        gram = None
        for slot in range(C):
            if slot < Y:
                for k in range(1, Y):
                    crossed(it, slot, k).wait_recv()
                value = y_sum[it, slot, 0]
                for y in range(1, Y):
                    value = value + y_sum[it, slot, y]
                if it > 0:
                    value = value * inv_root
                s_ref[it, slot] = value
                remote(
                    BULK, s_ref.at[it, slot], s_ref.at[it, Y + slot], s_recv_sem.at[it, slot], me_r, partner
                ).start()
                gram = square(value) if slot == 0 else gram + square(value)
                if slot == Y - 1:
                    gsend[it] = gram
                    for k in range(H):
                        h = far(k)
                        gram_copy(it, h, other).start()

                        @pl.when(me_r != base + h)
                        def _():
                            gram_copy(it, h, core).start()

                    grecv[it, 2 * R - 1] = gram
            else:
                landed(s_ref.at[it, slot], s_recv_sem.at[it, slot - Y])
                value = s_ref[it, slot]
            high = value.astype(jnp.bfloat16)
            low = (value - high.astype(jnp.float32)).astype(jnp.bfloat16)
            lhs[:K, :] = high
            lhs[K:, :] = low
            if slot < C - 1:
                product = jnp.dot(lhs[...], slab[slot * piece : (slot + 1) * piece, :], preferred_element_type=jnp.float32)
                product = product[:K] + product[K:]
                zacc[...] = product if slot == 0 else zacc[...] + product
        for w in range(W):
            cols = slice(w * wave, (w + 1) * wave)
            product = jnp.dot(lhs[...], slab[(C - 1) * piece :, cols], preferred_element_type=jnp.float32)
            product = zacc[:, cols] + product[:K] + product[K:]
            for h in range(H):
                zpart[it, w, h] = product[:, h * bw : (h + 1) * bw]
            for k in range(H):
                z_copy(it, w, far(k)).start()

        if it == 0:
            for i in TASKS[1]:
                turn(i)

        @pl.when(is_owner)
        def _():
            landed(grecv.at[it, pl.ds(0, 2 * R - 1)], g_recv_sem.at[it])
            total = grecv[it, 0]
            for r in range(1, 2 * R):
                total = total + grecv[it, r]
            _, inverse = factorize(total)
            own = me_r - base
            for w in range(W):
                if it == 0 and w == W - 1:
                    for i in TASKS[2]:
                        turn(i)
                landed(zrecv.at[it, w], z_recv_sem.at[it, w])
                total = zrecv[it, w, 0]
                for r in range(1, R):
                    total = total + zrecv[it, w, r]
                block_ref[it, w] = jnp.dot(
                    inverse, total, precision=HIGHEST, preferred_element_type=jnp.float32
                ).astype(jnp.bfloat16)
                for k in range(R):
                    back_copy(it, w, far_row(k), own).start()

        if it == 0:
            @pl.when(jnp.logical_not(is_owner))
            def _():
                for i in TASKS[2]:
                    turn(i)

            for i in TASKS[3]:
                turn(i)

    last = gathered(ITERS - 1)

    def to_partner(k):
        y = lax.rem(me_y + k, Y)
        return remote(BULK, fin_part.at[k], fin_recv.at[k], f_recv_sem.at[k], me_r, partner), y

    for k in list(range(1, Y)) + [0]:
        copy, y = to_partner(k)
        fin_part[k] = last(position(y * 2 + (core if k else other)))
        copy.start()
    for k in list(range(1, Y)) + [0]:
        y = lax.rem(me_y + k, Y)
        fin_send[k] = last(position(y * 2 + (other if k else core)))
    outer = []
    for k in range(1, Y):
        copy, y = to_partner(k)
        copy.wait_recv()
        fin_send[k] = fin_send[k] + fin_recv[k]
        copy = remote(BULK, fin_send.at[k], fin_y.at[k], fy_recv_sem.at[k - 1], me_r, y * 2 + other)
        copy.start()
        outer.append(copy)
    to_partner(0)[0].wait_recv()
    own = fin_send[0] + fin_recv[0]
    for k, copy in enumerate(outer):
        copy.wait_recv()
        own = own + fin_y[k + 1]
    own = own * inv_root
    fsend[...] = square(own)

    n = R * C

    def spread(k):
        pltpu.make_async_remote_copy(
            src_ref=fsend, dst_ref=frecv.at[n - 1 - k], send_sem=send_sem.at[LAST_GRAM],
            recv_sem=c_recv_sem.at[0], device_id=peer(k), device_id_type=MESH,
        ).start()

    repeat(1, n, spread)
    frecv[n - 1] = fsend[...]

    moved = ITERS * (C + Y * (Y - 1) + Y) * K * piece + ITERS * K * width + (2 * Y - 1) * K * piece
    sent_rows(BULK, moved, 4)
    sent(GRAM, frecv.at[pl.ds(0, ITERS * H)])

    @pl.when(is_owner)
    def _():
        sent(OWN_GRAM, frecv.at[pl.ds(0, ITERS * (H - 1))])
        sent_rows(BLOCK, ITERS * W * R * K * bw, 2)

    @pl.when(jnp.logical_not(is_owner))
    def _():
        sent(OWN_GRAM, frecv.at[pl.ds(0, ITERS * H)])

    landed(frecv.at[pl.ds(0, n - 1)], c_recv_sem.at[0])
    def held(d):
        return frecv[lax.rem(d - me - 1 + n, n)]

    parts = [held(d) for d in range(8)]
    for d in range(8, n):
        parts[d % 8] = parts[d % 8] + held(d)
    while len(parts) > 1:
        parts = [a + b for a, b in zip(parts[::2], parts[1::2])]
    upper, inverse = factorize(parts[0])
    ortho = jnp.dot(inverse, own, precision=HIGHEST, preferred_element_type=jnp.float32)
    basis_ref[...] = ortho * scale
    factor_ref[...] = upper / scale
    sent(LAST_GRAM, frecv.at[pl.ds(0, n - 1)])


def body(affinity, seed_values, sku_ids):
    R, C = lax.axis_size("row"), lax.axis_size("col")
    K = seed_values.shape[0]
    rows, width = affinity.shape
    piece, Y = rows // C, C // 2
    H = min(R // 2, width // LANES)
    W = 2 if width % (2 * H * LANES) == 0 else 1
    base, wave, bw = (R - H) // 2, width // W, width // W // H
    dims = (R, C, K, piece, width, base, H, W, 1.0 / math.sqrt(width * C), math.sqrt(rows * R))
    f32, bf16 = jnp.float32, jnp.bfloat16
    dma = pltpu.SemaphoreType.DMA
    vmem = pl.BlockSpec(memory_space=pltpu.VMEM)
    return pl.pallas_call(
        functools.partial(kernel, dims),
        out_shape=(
            pltpu.VMEM((K, piece), f32),
            pltpu.VMEM((K, K), f32),
        ),
        in_specs=[pl.BlockSpec(memory_space=pl.ANY)] * 3,
        out_specs=(vmem, vmem),
        scratch_shapes=[
            pltpu.VMEM((rows, width), bf16),
            pltpu.VMEM((C, width, piece), bf16),
            pltpu.SMEM((K,), jnp.int32),
            pltpu.VMEM((1, width), jnp.int32),
            pltpu.VMEM((K, width), bf16),
            pltpu.VMEM((C, K, piece), f32),
            pltpu.VMEM((ITERS, C, K, piece), f32),
            pltpu.VMEM((ITERS, C, K, piece), f32),
            pltpu.VMEM((ITERS, Y, K, piece), f32),
            pltpu.VMEM((ITERS, Y, Y, K, piece), f32),
            pltpu.VMEM((Y, K, piece), f32),
            pltpu.VMEM((Y, K, piece), f32),
            pltpu.VMEM((Y, K, piece), f32),
            pltpu.VMEM((Y, K, piece), f32),
            pltpu.VMEM((ITERS, C, K, piece), f32),
            pltpu.VMEM((2 * K, piece), bf16),
            pltpu.VMEM((K, width), f32),
            pltpu.VMEM((ITERS, W, H, K, bw), f32),
            pltpu.VMEM((ITERS, W, R, K, bw), f32),
            pltpu.VMEM((ITERS, W, K, bw), bf16),
            pltpu.VMEM((ITERS, W, K, wave), bf16),
            pltpu.VMEM((ITERS, K, K), f32),
            pltpu.VMEM((ITERS, 2 * R, K, K), f32),
            pltpu.VMEM((K, K), f32),
            pltpu.VMEM((R * C, K, K), f32),
            dma((DEPTH + 2,)),
            dma((5,)),
            dma((ITERS, C)),
            dma((ITERS, Y, Y - 1)),
            dma((Y,)),
            dma((Y - 1,)),
            dma((ITERS, Y)),
            dma((ITERS, W)),
            dma((ITERS, W)),
            dma((ITERS,)),
            dma((1,)),
        ],
        compiler_params=pltpu.CompilerParams(
            collective_id=0, has_side_effects=True, vmem_limit_bytes=60 * 1024 * 1024
        ),
    )(affinity, seed_values, sku_ids[None, :])


def solution(mesh):
    placed = (P("row", "col"), P(), P("col"))
    return jax.shard_map(
        body, mesh=mesh, in_specs=placed, out_specs=(P(None, ("row", "col")), P()), check_vma=False
    )
```

time: 61.2 us -> 56.6 us (0.925)
  the two profiles are of different devices: /device:TPU:15 before, /device:TPU:0 now
where the time goes in v3:
time: 56.6 us; the launch traced here: 55.5 us
  Pallas kernels  53.6 us (95%)
  local copies, waits for them, and re-layouts  1.23 us (2%)
  between operations  0.64 us (1%)
    pallas_call x1, Pallas kernels, body(): pl.pallas_call(functools.partial(kernel, dims), out_shape=(pltpu.VMEM((K,...  53.6 us
    unnamed x2, local copies, waits for them, and re-layouts  1.23 us

profile of v3, /device:TPU:0, one launch (start us, length us, event | category | flops | bytes accessed | tf_op | source)
XLA Modules:
  0.0 55.5 jit_solution(2620795326278426021)
XLA Ops:
  0.6 53.6 %shard_map.50 = (f32[16,1024]{1,0:T(8,128)S(1)}, f32[16,16]{1,0:T(8,128)S(1)}) custom-call(bf16[4096,2048]{1,0:T(8,128)(2,1)} %slab_hbm.1, s32[16]{0:T(128)} %seed_hbm.1, s32[1,2048]{1,0:T(1,128)} %bitcast.1), custom_call_target="tpu_custom_call" | custom-call | tf_op jit(solution)/shard_map/pallas_call | solution.py:417
  54.2 0.6 %copy.7 = f32[16,1024]{1,0:T(8,128)} copy(f32[16,1024]{1,0:T(8,128)S(1)} %get-tuple-element.2) | data formatting | bytes 131072
  54.9 0.6 %copy.8 = f32[16,16]{1,0:T(8,128)} copy(f32[16,16]{1,0:T(8,128)S(1)} %get-tuple-element.3) | data formatting | bytes 2048

commit v4 on v3

--- a/solution.py
+++ b/solution.py
@@ -10,6 +10,7 @@
 
 ITERS = 2
 SUB = 2
+CUT = 2
 DEPTH = 4
 LANES = 128
 TASKS = ((0, 1), (2, 3, 4), (5,), (6, 7))
@@ -43,22 +44,41 @@
     return (gauss / math.sqrt(total_columns)).astype(jnp.bfloat16)
 
 
-def factorize(gram):
+def refined_rsqrt(value):
+    root = lax.rsqrt(value)
+    return root * (1.5 - 0.5 * (value * root) * root)
+
+
+def factorize(gram, right):
     count = gram.shape[0]
-    rows = lax.broadcasted_iota(jnp.int32, (count, count), 0)
-    cols = lax.broadcasted_iota(jnp.int32, (count, count), 1)
-    left = gram
-    right = (rows == cols).astype(jnp.float32)
-    for j in range(count):
-        pivot = left[j : j + 1, j : j + 1]
-        inv = lax.rsqrt(pivot)
-        inv = inv * (1.5 - 0.5 * (pivot * inv) * inv)
-        left_row = left[j : j + 1, :] * inv
-        right_row = right[j : j + 1, :] * inv
-        factor = left[:, j : j + 1] * inv
-        left = jnp.where(rows == j, left_row, jnp.where(rows > j, left - factor * left_row, left))
-        right = jnp.where(rows == j, right_row, jnp.where(rows > j, right - factor * right_row, right))
-    return jnp.where(rows <= cols, left, 0.0), right
+    shape = (count, LANES)
+    rows = lax.broadcasted_iota(jnp.int32, shape, 0)
+    cols = lax.broadcasted_iota(jnp.int32, shape, 1)
+    top = jnp.max(jnp.max(gram, axis=1, keepdims=True), axis=0, keepdims=True)
+    scale = refined_rsqrt(top)
+    left = jnp.concatenate([gram * (1.0 / top), jnp.zeros((count, LANES - count), jnp.float32)], axis=1)
+    arrays = [left] + list(right)
+    results = [jnp.zeros(shape, jnp.float32) for _ in arrays]
+    for j in range(0, count, 2):
+        first = jnp.broadcast_to(arrays[0][:, j : j + 1], shape)
+        second = jnp.broadcast_to(arrays[0][:, j + 1 : j + 2], shape)
+        a, b, c = first[j : j + 1], first[j + 1 : j + 2], second[j + 1 : j + 2]
+        det = a * c - b * b
+        inv = 1.0 / det
+        below = rows > j + 1
+        one = jnp.where(below, first * c - second * b, 0.0) * inv
+        two = jnp.where(below, second * a - first * b, 0.0) * inv
+        root = refined_rsqrt(a)
+        next_root = refined_rsqrt(det) * (a * root)
+        ratio = b * root * root
+        for i, array in enumerate(arrays):
+            head, tail = array[j : j + 1], array[j + 1 : j + 2]
+            results[i] = jnp.where(
+                rows == j, head * root, jnp.where(rows == j + 1, (tail - ratio * head) * next_root, results[i])
+            )
+            arrays[i] = array - (one * head + two * tail)
+    upper = jnp.where(rows <= cols, results[0], 0.0) * (top * scale)
+    return upper[:, :count], [array * scale for array in results[1:]]
 
 
 def repeat(start, stop, step):
@@ -100,7 +120,7 @@
     def far_row(k):
         return (R - 1 - k) + flip * (2 * k - R + 1)
 
-    span = piece // SUB
+    span, unit, units = piece // SUB, piece // CUT, C * CUT
     n_load = C * SUB
 
     def load(i):
@@ -218,9 +238,11 @@
     for it in range(ITERS):
         def hand_over(q):
             swapped(it, Y + q).wait_recv()
-            y_send[it, q] = part[it, Y + q] + half_recv[it, Y + q]
-            for k in range(1, Y):
-                cross(it, q, k).start()
+            for u in range(CUT):
+                here = slice(u * unit, (u + 1) * unit)
+                y_send[it, q * CUT + u] = part[it, Y + q, :, here] + half_recv[it, Y + q, :, here]
+                for k in range(1, Y):
+                    cross(it, q * CUT + u, k).start()
 
         if it == 0:
             for i in range(n_load):
@@ -243,31 +265,35 @@
                 turn(i)
         else:
             last = gathered(it - 1)
-            for slot in range(C):
-                part[it, slot] = last(slot)
-                swap(it, slot).start()
             for q in range(Y):
-                hand_over(q)
+                for slot in (q, Y + q):
+                    part[it, slot] = last(slot)
+                    swap(it, slot).start()
+                    if q > 0 and slot == q:
+                        hand_over(q - 1)
+            hand_over(Y - 1)
         for q in range(Y):
             swapped(it, q).wait_recv()
-            y_sum[it, q, me_y] = part[it, q] + half_recv[it, q]
+            for u in range(CUT):
+                here = slice(u * unit, (u + 1) * unit)
+                y_sum[it, q * CUT + u, me_y] = part[it, q, :, here] + half_recv[it, q, :, here]
 
         gram = None
-        for slot in range(C):
-            if slot < Y:
+        for n in range(units):
+            if n < units // 2:
                 for k in range(1, Y):
-                    crossed(it, slot, k).wait_recv()
-                value = y_sum[it, slot, 0]
+                    crossed(it, n, k).wait_recv()
+                value = y_sum[it, n, 0]
                 for y in range(1, Y):
-                    value = value + y_sum[it, slot, y]
+                    value = value + y_sum[it, n, y]
                 if it > 0:
                     value = value * inv_root
-                s_ref[it, slot] = value
+                s_ref[it, n] = value
                 remote(
-                    BULK, s_ref.at[it, slot], s_ref.at[it, Y + slot], s_recv_sem.at[it, slot], me_r, partner
+                    BULK, s_ref.at[it, n], s_ref.at[it, units // 2 + n], s_recv_sem.at[it, n], me_r, partner
                 ).start()
-                gram = square(value) if slot == 0 else gram + square(value)
-                if slot == Y - 1:
+                gram = square(value) if n == 0 else gram + square(value)
+                if n == units // 2 - 1:
                     gsend[it] = gram
                     for k in range(H):
                         h = far(k)
@@ -279,19 +305,23 @@
 
                     grecv[it, 2 * R - 1] = gram
             else:
-                landed(s_ref.at[it, slot], s_recv_sem.at[it, slot - Y])
-                value = s_ref[it, slot]
+                landed(s_ref.at[it, n], s_recv_sem.at[it, n - units // 2])
+                value = s_ref[it, n]
             high = value.astype(jnp.bfloat16)
             low = (value - high.astype(jnp.float32)).astype(jnp.bfloat16)
-            lhs[:K, :] = high
-            lhs[K:, :] = low
-            if slot < C - 1:
-                product = jnp.dot(lhs[...], slab[slot * piece : (slot + 1) * piece, :], preferred_element_type=jnp.float32)
+            lhs[n % 2, :K, :] = high
+            lhs[n % 2, K:, :] = low
+            if n < units - 1:
+                product = jnp.dot(
+                    lhs[n % 2], slab[n * unit : (n + 1) * unit, :], preferred_element_type=jnp.float32
+                )
                 product = product[:K] + product[K:]
-                zacc[...] = product if slot == 0 else zacc[...] + product
+                zacc[...] = product if n == 0 else zacc[...] + product
         for w in range(W):
             cols = slice(w * wave, (w + 1) * wave)
-            product = jnp.dot(lhs[...], slab[(C - 1) * piece :, cols], preferred_element_type=jnp.float32)
+            product = jnp.dot(
+                lhs[(units - 1) % 2], slab[(units - 1) * unit :, cols], preferred_element_type=jnp.float32
+            )
             product = zacc[:, cols] + product[:K] + product[K:]
             for h in range(H):
                 zpart[it, w, h] = product[:, h * bw : (h + 1) * bw]
@@ -308,7 +338,8 @@
             total = grecv[it, 0]
             for r in range(1, 2 * R):
                 total = total + grecv[it, r]
-            _, inverse = factorize(total)
+            identity = lax.broadcasted_iota(jnp.int32, (K, LANES), 0) == lax.broadcasted_iota(jnp.int32, (K, LANES), 1)
+            inverse = factorize(total, [identity.astype(jnp.float32)])[1][0][:, :K]
             own = me_r - base
             for w in range(W):
                 if it == 0 and w == W - 1:
@@ -395,9 +426,10 @@
         parts[d % 8] = parts[d % 8] + held(d)
     while len(parts) > 1:
         parts = [a + b for a, b in zip(parts[::2], parts[1::2])]
-    upper, inverse = factorize(parts[0])
-    ortho = jnp.dot(inverse, own, precision=HIGHEST, preferred_element_type=jnp.float32)
-    basis_ref[...] = ortho * scale
+    chunks = [slice(i, i + LANES) for i in range(0, piece, LANES)]
+    upper, ortho = factorize(parts[0], [own[:, chunk] for chunk in chunks])
+    for chunk, array in zip(chunks, ortho):
+        basis_ref[:, chunk] = array * scale
     factor_ref[...] = upper / scale
     sent(LAST_GRAM, frecv.at[pl.ds(0, n - 1)])
 
@@ -408,7 +440,7 @@
     rows, width = affinity.shape
     piece, Y = rows // C, C // 2
     H = min(R // 2, width // LANES)
-    W = 2 if width % (2 * H * LANES) == 0 else 1
+    W = 4 if width % (4 * H * LANES) == 0 else 1
     base, wave, bw = (R - H) // 2, width // W, width // W // H
     dims = (R, C, K, piece, width, base, H, W, 1.0 / math.sqrt(width * C), math.sqrt(rows * R))
     f32, bf16 = jnp.float32, jnp.bfloat16
@@ -431,14 +463,14 @@
             pltpu.VMEM((C, K, piece), f32),
             pltpu.VMEM((ITERS, C, K, piece), f32),
             pltpu.VMEM((ITERS, C, K, piece), f32),
-            pltpu.VMEM((ITERS, Y, K, piece), f32),
-            pltpu.VMEM((ITERS, Y, Y, K, piece), f32),
+            pltpu.VMEM((ITERS, Y * CUT, K, piece // CUT), f32),
+            pltpu.VMEM((ITERS, Y * CUT, Y, K, piece // CUT), f32),
             pltpu.VMEM((Y, K, piece), f32),
             pltpu.VMEM((Y, K, piece), f32),
             pltpu.VMEM((Y, K, piece), f32),
             pltpu.VMEM((Y, K, piece), f32),
-            pltpu.VMEM((ITERS, C, K, piece), f32),
-            pltpu.VMEM((2 * K, piece), bf16),
+            pltpu.VMEM((ITERS, C * CUT, K, piece // CUT), f32),
+            pltpu.VMEM((2, 2 * K, piece // CUT), bf16),
             pltpu.VMEM((K, width), f32),
             pltpu.VMEM((ITERS, W, H, K, bw), f32),
             pltpu.VMEM((ITERS, W, R, K, bw), f32),
@@ -451,10 +483,10 @@
             dma((DEPTH + 2,)),
             dma((5,)),
             dma((ITERS, C)),
-            dma((ITERS, Y, Y - 1)),
+            dma((ITERS, Y * CUT, Y - 1)),
             dma((Y,)),
             dma((Y - 1,)),
-            dma((ITERS, Y)),
+            dma((ITERS, Y * CUT)),
             dma((ITERS, W)),
             dma((ITERS, W)),
             dma((ITERS,)),

time: 56.6 us -> 55.3 us (0.977)
  Pallas kernels: 53.6 us -> 52.5 us
    pallas_call x1, Pallas kernels: 53.6 us -> 52.5 us  [body(): pl.pallas_call(functools.partial(kernel, dims), out_shape=(pltpu.VMEM((K,...]
where the time goes in v4:
time: 55.3 us; the launch traced here: 54.4 us
  Pallas kernels  52.5 us (95%)
  local copies, waits for them, and re-layouts  1.23 us (2%)
  between operations  0.64 us (1%)
    pallas_call x1, Pallas kernels, body(): pl.pallas_call(functools.partial(kernel, dims), out_shape=(pltpu.VMEM((K,...  52.5 us
    unnamed x2, local copies, waits for them, and re-layouts  1.23 us

profile of v4, /device:TPU:0, one launch (start us, length us, event | category | flops | bytes accessed | tf_op | source)
XLA Modules:
  0.0 54.4 jit_solution(9926332926588269018)
XLA Ops:
  0.6 52.5 %shard_map.50 = (f32[16,1024]{1,0:T(8,128)S(1)}, f32[16,16]{1,0:T(8,128)S(1)}) custom-call(bf16[4096,2048]{1,0:T(8,128)(2,1)} %slab_hbm.1, s32[16]{0:T(128)} %seed_hbm.1, s32[1,2048]{1,0:T(1,128)} %bitcast.1), custom_call_target="tpu_custom_call" | custom-call | tf_op jit(solution)/shard_map/pallas_call | solution.py:449
  53.1 0.6 %copy.7 = f32[16,1024]{1,0:T(8,128)} copy(f32[16,1024]{1,0:T(8,128)S(1)} %get-tuple-element.2) | data formatting | bytes 131072
  53.8 0.6 %copy.8 = f32[16,16]{1,0:T(8,128)} copy(f32[16,16]{1,0:T(8,128)S(1)} %get-tuple-element.3) | data formatting | bytes 2048

commit v5 on v4

--- a/solution.py
+++ b/solution.py
@@ -434,6 +434,17 @@
     sent(LAST_GRAM, frecv.at[pl.ds(0, n - 1)])
 
 
+def put_out(basis_ref, factor_ref, basis_out, factor_out, sem):
+    copies = [
+        pltpu.make_async_copy(basis_ref, basis_out, sem.at[0]),
+        pltpu.make_async_copy(factor_ref, factor_out, sem.at[1]),
+    ]
+    for copy in copies:
+        copy.start()
+    for copy in copies:
+        copy.wait()
+
+
 def body(affinity, seed_values, sku_ids):
     R, C = lax.axis_size("row"), lax.axis_size("col")
     K = seed_values.shape[0]
@@ -446,7 +457,7 @@
     f32, bf16 = jnp.float32, jnp.bfloat16
     dma = pltpu.SemaphoreType.DMA
     vmem = pl.BlockSpec(memory_space=pltpu.VMEM)
-    return pl.pallas_call(
+    results = pl.pallas_call(
         functools.partial(kernel, dims),
         out_shape=(
             pltpu.VMEM((K, piece), f32),
@@ -496,6 +507,13 @@
             collective_id=0, has_side_effects=True, vmem_limit_bytes=60 * 1024 * 1024
         ),
     )(affinity, seed_values, sku_ids[None, :])
+    return pl.pallas_call(
+        put_out,
+        out_shape=tuple(jax.ShapeDtypeStruct(array.shape, f32) for array in results),
+        in_specs=[vmem, vmem],
+        out_specs=(pl.BlockSpec(memory_space=pl.ANY),) * 2,
+        scratch_shapes=[dma((2,))],
+    )(*[pltpu.with_memory_space_constraint(array, pltpu.VMEM) for array in results])
 
 
 def solution(mesh):

time: 55.3 us -> 54.9 us (level)
  local copies, waits for them, and re-layouts: 1.23 us -> 0 us
  Pallas kernels: 52.5 us -> 53.2 us
    unnamed x2 -> x0, local copies, waits for them, and re-layouts: 1.23 us -> none
    pallas_call x0 -> x1, Pallas kernels: none -> 0.65 us  [body(): pl.pallas_call(put_out, out_shape=tuple((jax.ShapeDtypeStruct(array.shape...]
where the time goes in v5:
time: 54.9 us; the launch traced here: 54 us
  Pallas kernels  53.2 us (97%)
  between operations  0.8 us (1%)
    pallas_call x1, Pallas kernels, body(): pl.pallas_call(functools.partial(kernel, dims), out_shape=(pltpu.VMEM((K,...  52.5 us

profile of v5, /device:TPU:0, one launch (start us, length us, event | category | flops | bytes accessed | tf_op | source)
XLA Modules:
  0.0 54.0 jit_solution(13357014335982973813)
XLA Ops:
  0.6 52.5 %shard_map.50 = (f32[16,1024]{1,0:T(8,128)S(1)}, f32[16,16]{1,0:T(8,128)S(1)}) custom-call(bf16[4096,2048]{1,0:T(8,128)(2,1)} %slab_hbm.1, s32[16]{0:T(128)} %seed_hbm.1, s32[1,2048]{1,0:T(1,128)} %bitcast.1), custom_call_target="tpu_custom_call" | custom-call | tf_op jit(solution)/shard_map/pallas_call | solution.py:460
  53.1 0.7 %shard_map.51 = (f32[16,1024]{1,0:T(8,128)}, f32[16,16]{1,0:T(8,128)}) custom-call(f32[16,1024]{1,0:T(8,128)S(1)} %get-tuple-element.4.basis_ref, f32[16,16]{1,0:T(8,128)S(1)} %get-tuple-element.5.factor_ref), custom_call_target="tpu_custom_call" | custom-call | tf_op jit(solution)/shard_map/pallas_call | solution.py:510

commit v6 on v5

--- a/solution.py
+++ b/solution.py
@@ -183,10 +183,10 @@
 
     def swap(it, slot):
         there = (slot + Y) % C
-        return remote(BULK, part.at[it, slot], half_recv.at[it, there], a_recv_sem.at[it, there], me_r, partner)
+        return remote(BULK, part.at[it, slot], half_recv.at[it, there], a_recv_sem.at[there], me_r, partner)
 
     def swapped(it, slot):
-        return remote(BULK, part.at[it, slot], half_recv.at[it, slot], a_recv_sem.at[it, slot], me_r, partner)
+        return remote(BULK, part.at[it, slot], half_recv.at[it, slot], a_recv_sem.at[slot], me_r, partner)
 
     def cross(it, q, k):
         y = lax.rem(me_y + k, Y)
@@ -211,11 +211,11 @@
         )
 
     def z_copy(it, w, h):
-        return remote(BULK, zpart.at[it, w, h], zrecv.at[it, w, me_r], z_recv_sem.at[it, w], base + h, partner)
+        return remote(BULK, zpart.at[it, w, h], zrecv.at[it, w, me_r], z_recv_sem.at[w], base + h, partner)
 
     def back_copy(it, w, row, h):
         cols = pl.ds(pl.multiple_of(h * bw, bw), bw)
-        return remote(BLOCK, block_ref.at[it, w], back.at[it, w, :, cols], b_recv_sem.at[it, w], row, partner)
+        return remote(BLOCK, block_ref.at[it, w], back.at[it, w, :, cols], b_recv_sem.at[w], row, partner)
 
     def landed(ref, sem):
         remote(BULK, ref, ref, sem, me_r, partner).wait_recv()
@@ -226,7 +226,7 @@
             return jnp.dot(back[it, w], slab_t[slot, rows, :], preferred_element_type=jnp.float32)
 
         for w in range(W):
-            landed(back.at[it, w], b_recv_sem.at[it, w])
+            landed(back.at[it, w], b_recv_sem.at[w])
             if w < W - 1:
                 for slot in range(C):
                     value = product(w, slot)
@@ -290,7 +290,7 @@
                     value = value * inv_root
                 s_ref[it, n] = value
                 remote(
-                    BULK, s_ref.at[it, n], s_ref.at[it, units // 2 + n], s_recv_sem.at[it, n], me_r, partner
+                    BULK, s_ref.at[it, n], s_ref.at[it, units // 2 + n], s_recv_sem.at[n], me_r, partner
                 ).start()
                 gram = square(value) if n == 0 else gram + square(value)
                 if n == units // 2 - 1:
@@ -305,7 +305,7 @@
 
                     grecv[it, 2 * R - 1] = gram
             else:
-                landed(s_ref.at[it, n], s_recv_sem.at[it, n - units // 2])
+                landed(s_ref.at[it, n], s_recv_sem.at[n - units // 2])
                 value = s_ref[it, n]
             high = value.astype(jnp.bfloat16)
             low = (value - high.astype(jnp.float32)).astype(jnp.bfloat16)
@@ -345,7 +345,7 @@
                 if it == 0 and w == W - 1:
                     for i in TASKS[2]:
                         turn(i)
-                landed(zrecv.at[it, w], z_recv_sem.at[it, w])
+                landed(zrecv.at[it, w], z_recv_sem.at[w])
                 total = zrecv[it, w, 0]
                 for r in range(1, R):
                     total = total + zrecv[it, w, r]
@@ -493,13 +493,13 @@
             pltpu.VMEM((R * C, K, K), f32),
             dma((DEPTH + 2,)),
             dma((5,)),
-            dma((ITERS, C)),
+            dma((C,)),
             dma((ITERS, Y * CUT, Y - 1)),
             dma((Y,)),
             dma((Y - 1,)),
-            dma((ITERS, Y * CUT)),
-            dma((ITERS, W)),
-            dma((ITERS, W)),
+            dma((Y * CUT,)),
+            dma((W,)),
+            dma((W,)),
             dma((ITERS,)),
             dma((1,)),
         ],

time: 54.9 us -> 54.7 us (level)
  no operation moved by 1% of the time
where the time goes in v6:
time: 54.7 us; the launch traced here: 53.8 us
  Pallas kernels  53 us (97%)
  between operations  0.8 us (1%)
    pallas_call x1, Pallas kernels, body(): pl.pallas_call(functools.partial(kernel, dims), out_shape=(pltpu.VMEM((K,...  52.4 us

profile of v6, /device:TPU:0, one launch (start us, length us, event | category | flops | bytes accessed | tf_op | source)
XLA Modules:
  0.0 53.8 jit_solution(10875604230822496045)
XLA Ops:
  0.6 52.4 %shard_map.50 = (f32[16,1024]{1,0:T(8,128)S(1)}, f32[16,16]{1,0:T(8,128)S(1)}) custom-call(bf16[4096,2048]{1,0:T(8,128)(2,1)} %slab_hbm.1, s32[16]{0:T(128)} %seed_hbm.1, s32[1,2048]{1,0:T(1,128)} %bitcast.1), custom_call_target="tpu_custom_call" | custom-call | tf_op jit(solution)/shard_map/pallas_call | solution.py:460
  53.0 0.7 %shard_map.51 = (f32[16,1024]{1,0:T(8,128)}, f32[16,16]{1,0:T(8,128)}) custom-call(f32[16,1024]{1,0:T(8,128)S(1)} %get-tuple-element.4.basis_ref, f32[16,16]{1,0:T(8,128)S(1)} %get-tuple-element.5.factor_ref), custom_call_target="tpu_custom_call" | custom-call | tf_op jit(solution)/shard_map/pallas_call | solution.py:510

commit v7 on v6

--- a/solution.py
+++ b/solution.py
@@ -401,7 +401,7 @@
             recv_sem=c_recv_sem.at[0], device_id=peer(k), device_id_type=MESH,
         ).start()
 
-    repeat(1, n, spread)
+    repeat(1, n, lambda k: spread(n - k))
     frecv[n - 1] = fsend[...]
 
     moved = ITERS * (C + Y * (Y - 1) + Y) * K * piece + ITERS * K * width + (2 * Y - 1) * K * piece

time: 54.7 us -> 57.4 us (1.049); the launches traced: 53.8 us -> 57.3 us
  Pallas kernels: 53 us -> 56.5 us
    pallas_call x1, Pallas kernels: 52.4 us -> 55.8 us  [body(): pl.pallas_call(functools.partial(kernel, dims), out_shape=(pltpu.VMEM((K,...]
where the time goes in v7:
time: 57.4 us; the launch traced here: 57.3 us
  Pallas kernels  56.5 us (98%)
  between operations  0.8 us (1%)
    pallas_call x1, Pallas kernels, body(): pl.pallas_call(functools.partial(kernel, dims), out_shape=(pltpu.VMEM((K,...  55.8 us

profile of v7, /device:TPU:0, one launch (start us, length us, event | category | flops | bytes accessed | tf_op | source)
XLA Modules:
  0.0 57.3 jit_solution(17172893631844414356)
XLA Ops:
  0.6 55.8 %shard_map.50 = (f32[16,1024]{1,0:T(8,128)S(1)}, f32[16,16]{1,0:T(8,128)S(1)}) custom-call(bf16[4096,2048]{1,0:T(8,128)(2,1)} %slab_hbm.1, s32[16]{0:T(128)} %seed_hbm.1, s32[1,2048]{1,0:T(1,128)} %bitcast.1), custom_call_target="tpu_custom_call" | custom-call | tf_op jit(solution)/shard_map/pallas_call | solution.py:460
  56.4 0.7 %shard_map.51 = (f32[16,1024]{1,0:T(8,128)}, f32[16,16]{1,0:T(8,128)}) custom-call(f32[16,1024]{1,0:T(8,128)S(1)} %get-tuple-element.4.basis_ref, f32[16,16]{1,0:T(8,128)S(1)} %get-tuple-element.5.factor_ref), custom_call_target="tpu_custom_call" | custom-call | tf_op jit(solution)/shard_map/pallas_call | solution.py:510
